TPU v7x, 128 devices: a whole 4x4x4 slice. The times are simulated.
128 devices in a mesh: pipe: 8 (over y, core), seq: 16 (over z, x).
Axes of the slice: x: 4, y: 4, z: 4, core: 2. Of those that a mesh axis runs over, the one named last changes fastest.
Arguments:
- hidden: bfloat16 [2, 384, 3072], P(None, 'seq'), may hold values from -8 to 8
- mod_shift: float32 [8, 3072], P('pipe'), may hold values from -0.3 to 0.3
- mod_scale: float32 [8, 3072], P('pipe'), may hold values from -3 to 3
- mod_gate: float32 [8, 3072], P('pipe'), may hold values from 0.5 to 2.5
- norm_gain: float32 [8, 2, 128], P('pipe'), may hold values from 0.5 to 1.5
- input_proj: bfloat16 [8, 3072, 3, 2048], P('pipe', None, None, 'seq'), may hold values from -0.109375 to 0.109375
- output_proj: bfloat16 [8, 2048, 3072], P('pipe', 'seq'), may hold values from -0.5 to 0.5
- stale_cache: bfloat16 [8, 2, 384, 2, 2048], P('pipe', None, 'seq'), may hold values from -6 to 6
Outputs:
- block_output: bfloat16 [8, 2, 384, 3072], P('pipe', None, 'seq')
- fresh_cache: bfloat16 [8, 2, 384, 2, 2048], P('pipe', None, 'seq')
All inputs are finite; a program needn't handle non-finite values.
Results may differ from a plain program's by a relative error of at most 0.019.
Values may be sent and summed in bfloat16 or wider, within the bound.
A program may use at most 64 MiB of HBM per device.

v0:
```python
import math

import jax
import jax.numpy as jnp
from jax import lax
from jax.sharding import PartitionSpec as P


def from_everyone(array, axis):
    copies = jnp.broadcast_to(array, (lax.axis_size(axis), *array.shape))
    return lax.all_to_all(copies, axis, split_axis=0, concat_axis=0, tiled=True)


def in_order(parts, dim):
    parts = jnp.moveaxis(parts, 0, dim)
    lengths = parts.shape
    return parts.reshape(*lengths[:dim], lengths[dim] * lengths[dim + 1], *lengths[dim + 2 :])


def collect(array, axis, dim):
    parts = from_everyone(array, axis)
    return in_order(parts, dim)


def shifted(value, axis, steps):
    count = lax.axis_size(axis)
    first, last = (max(0, -steps), min(count, count - steps))
    return lax.ppermute(value, axis, [(source, source + steps) for source in range(first, last)])


def layer_norm(values, shift_row, scale_row):
    widened = values.astype(jnp.float32)
    centered = widened - jnp.mean(widened, axis=-1, keepdims=True)
    spread = jnp.mean(centered * centered, axis=-1, keepdims=True)
    return (centered / jnp.sqrt(spread + 1e-06) * (1.0 + scale_row) + shift_row).astype(
        jnp.bfloat16
    )


def head_norm(values, gain_row, head_size):
    row_count = values.shape[0]
    split = values.reshape(row_count, values.shape[1] // head_size, head_size)
    square = jnp.mean(split * split, axis=-1, keepdims=True)
    return (
        (split / jnp.sqrt(square + 1e-06) * gain_row)
        .reshape(row_count, values.shape[1])
        .astype(jnp.bfloat16)
    )


def attend(queries, own_keys, own_values, far_keys, far_values, head_size):
    row_count = queries.shape[0]
    head_count = queries.shape[1] // head_size
    shaped = lambda array: array.reshape(array.shape[0], head_count, head_size)
    query_heads = shaped(queries)
    factor = 1.0 / math.sqrt(head_size)
    near_scores = (
        jnp.einsum(
            "thd,shd->hts", query_heads, shaped(own_keys), preferred_element_type=jnp.float32
        )
        * factor
    )
    far_scores = (
        jnp.einsum(
            "thd,shd->hts", query_heads, shaped(far_keys), preferred_element_type=jnp.float32
        )
        * factor
    )
    near_exp = jnp.exp(near_scores)
    far_exp = jnp.exp(far_scores)
    denominator = jnp.sum(near_exp, axis=-1, keepdims=True) + jnp.sum(
        far_exp, axis=-1, keepdims=True
    )
    near_prob = (near_exp / denominator).astype(jnp.bfloat16)
    far_prob = (far_exp / denominator).astype(jnp.bfloat16)
    mixed = jnp.einsum(
        "hts,shd->thd", near_prob, shaped(own_values), preferred_element_type=jnp.float32
    )
    mixed = mixed + jnp.einsum(
        "hts,shd->thd", far_prob, shaped(far_values), preferred_element_type=jnp.float32
    )
    return mixed.reshape(row_count, head_count * head_size).astype(jnp.bfloat16)


def body(hidden, mod_shift, mod_scale, mod_gate, norm_gain, input_proj, output_proj, stale_cache):
    sections = lax.axis_size("pipe")
    section = lax.axis_index("pipe")
    patch_count = hidden.shape[0]
    turn_count = patch_count + sections - 1
    local_rows = hidden.shape[1]
    model_width = hidden.shape[2]
    head_size = norm_gain.shape[2]
    channels = input_proj.shape[3]
    patch_rows = local_rows * lax.axis_size("seq")
    weight_flat = input_proj[0].reshape(model_width, 3 * channels)
    shift_row = mod_shift[0]
    scale_row = mod_scale[0]
    gate_row = mod_gate[0]
    far_local = stale_cache[0, 1]
    far_stale = lax.all_to_all(far_local, "seq", split_axis=2, concat_axis=0, tiled=True)
    out_full = lax.all_gather(output_proj[0], "seq", axis=0, tiled=True)

    def project(block_rows):
        return jnp.dot(block_rows, weight_flat, preferred_element_type=jnp.float32)

    def turn_step(turn_index, carry):
        incoming, outputs, cache_store = carry
        raw_slot = turn_index - section
        usable = (raw_slot >= 0) & (raw_slot < patch_count)
        slot_index = jnp.clip(raw_slot, 0, 1)
        source = lax.dynamic_index_in_dim(hidden, slot_index, 0, keepdims=False)
        current = jnp.where(section == 0, source, incoming)
        normed = layer_norm(current, shift_row, scale_row)
        projected = project(collect(normed, "seq", 0))
        queries = head_norm(projected[:, :channels], norm_gain[0, 0], head_size)
        fresh_keys = head_norm(projected[:, channels : 2 * channels], norm_gain[0, 1], head_size)
        values = projected[:, 2 * channels :].astype(jnp.bfloat16)
        fresh_pair = jnp.stack([fresh_keys, values], axis=1)
        far_pair = jnp.where(slot_index == 0, far_stale, cache_store[0])
        attended = attend(queries, fresh_keys, values, far_pair[:, 0], far_pair[:, 1], head_size)
        regrouped = lax.all_to_all(attended, "seq", split_axis=0, concat_axis=1, tiled=True)
        update = jnp.dot(regrouped, out_full, preferred_element_type=jnp.float32)
        result = (current.astype(jnp.float32) + gate_row * update).astype(jnp.bfloat16)
        for position in range(patch_count):
            taken = usable & (slot_index == position)
            outputs = outputs.at[position].set(jnp.where(taken, result, outputs[position]))
            cache_store = cache_store.at[position].set(
                jnp.where(taken, fresh_pair, cache_store[position])
            )
        incoming = shifted(result, "pipe", 1)
        return (incoming, outputs, cache_store)

    start_carry = (
        jnp.zeros((local_rows, model_width), jnp.bfloat16),
        jnp.zeros((patch_count, local_rows, model_width), jnp.bfloat16),
        jnp.zeros((patch_count, patch_rows, 2, channels), jnp.bfloat16),
    )
    incoming, outputs, cache_store = lax.fori_loop(0, turn_count, turn_step, start_carry)
    regrouped_cache = lax.all_to_all(cache_store, "seq", split_axis=1, concat_axis=3, tiled=True)
    return (outputs[None], regrouped_cache[None])


def solution(mesh):
    in_specs = (
        P(None, "seq", None),
        P("pipe", None),
        P("pipe", None),
        P("pipe", None),
        P("pipe", None, None),
        P("pipe", None, None, "seq"),
        P("pipe", "seq", None),
        P("pipe", None, "seq", None, None),
    )
    out_specs = (P("pipe", None, "seq", None), P("pipe", None, "seq", None, None))
    return jax.shard_map(body, mesh=mesh, in_specs=in_specs, out_specs=out_specs, check_vma=False)
```

profile of v0, /device:TPU:25, one launch (start us, length us, event | category | flops | bytes accessed | tf_op | source)
XLA Modules:
  0.0 726.9 jit_solution(18128173824709693681)
XLA Ops:
  12.6 7.6 %all-to-all-start.2 = ((bf16[16,2,3072]{2,1,0:T(2,128)(2,1)}), bf16[16,2,3072]{2,1,0:T(2,128)(2,1)S(1)}, u32[]{:S(2)}, u32[]{:S(2)}) async-start(bf16[16,2,3072]{2,1,0:T(2,128)(2,1)} %reshape.490), calls=%async_computation.2 | async-start | bytes 393216 | tf_op jit(solution)/shard_map/all_to_all | solution.py:100
  29.7 72.3 %all-gather.3.cloned.1.call-done = bf16[1,2048,3072]{2,1,0:T(8,128)(2,1)} async-done(((bf16[1,128,3072]{2,1,0:T(8,128)(2,1)}), bf16[1,2048,3072]{2,1,0:T(8,128)(2,1)}) %all-gather.3.cloned.1.call-update) | async-done | bytes 12582928 | tf_op jit(solution)/shard_map/all_gather | solution.py:101
  102.1 605.2 %while.24 = (s32[]{:T(128)}, bf16[24,3072]{1,0:T(8,128)(2,1)S(1)}, bf16[2,24,3072]{2,1,0:T(8,128)(2,1)S(1)}, bf16[2,384,2,128]{1,3,2,0:T(8,128)(2,1)S(1)}, pred[...) while((s32[]{:T(128)}, bf16[24,3072]{1,0:T(8,128)(2,1)S(1)}, ...), condition=%wide.region_7.8_spmd, body=%wide.region_0.7_spmd.sunk | while | flops 1363504640 | bytes 38239548 | solution.py:138
  112.3 32.4 %all-to-all-done = bf16[16,24,3072]{2,1,0:T(8,128)(2,1)S(1)} async-done(((bf16[16,24,3072]{2,1,0:T(8,128)(2,1)}), bf16[16,24,3072]{2,1,0:T(8,128)(2,1)S(1)}, u32[]{:S(2)}, u32[]{:S(2)}) %all-to-all-start) | async-done | bytes 2359328 | tf_op jit(solution)/shard_map/while/body/eval_jaxpr/all_to_all | solution.py:11
  181.5 25.4 %all-to-all-done = bf16[16,24,3072]{2,1,0:T(8,128)(2,1)S(1)} async-done(((bf16[16,24,3072]{2,1,0:T(8,128)(2,1)}), bf16[16,24,3072]{2,1,0:T(8,128)(2,1)S(1)}, u32[]{:S(2)}, u32[]{:S(2)}) %all-to-all-start) | async-done | bytes 2359328 | tf_op jit(solution)/shard_map/while/body/eval_jaxpr/all_to_all | solution.py:11
  212.5 8.0 %all-to-all-start.1 = ((bf16[16,24,128]{2,1,0:T(8,128)(2,1)}), bf16[16,24,128]{2,1,0:T(8,128)(2,1)S(1)}, u32[]{:S(2)}, u32[]{:S(2)}) async-start(bf16[16,24,128]{2,1,0:T(8,128)(2,1)} %bitcast.121), calls=%async_computation.1 | async-start | bytes 196608 | tf_op jit(solution)/shard_map/while/body/eval_jaxpr/all_to_all | solution.py:121
  220.7 6.5 all-to-all-done.1
  248.4 25.3 %all-to-all-done = bf16[16,24,3072]{2,1,0:T(8,128)(2,1)S(1)} async-done(((bf16[16,24,3072]{2,1,0:T(8,128)(2,1)}), bf16[16,24,3072]{2,1,0:T(8,128)(2,1)S(1)}, u32[]{:S(2)}, u32[]{:S(2)}) %all-to-all-start) | async-done | bytes 2359328 | tf_op jit(solution)/shard_map/while/body/eval_jaxpr/all_to_all | solution.py:11
  279.3 7.9 %all-to-all-start.1 = ((bf16[16,24,128]{2,1,0:T(8,128)(2,1)}), bf16[16,24,128]{2,1,0:T(8,128)(2,1)S(1)}, u32[]{:S(2)}, u32[]{:S(2)}) async-start(bf16[16,24,128]{2,1,0:T(8,128)(2,1)} %bitcast.121), calls=%async_computation.1 | async-start | bytes 196608 | tf_op jit(solution)/shard_map/while/body/eval_jaxpr/all_to_all | solution.py:121
  315.4 25.4 %all-to-all-done = bf16[16,24,3072]{2,1,0:T(8,128)(2,1)S(1)} async-done(((bf16[16,24,3072]{2,1,0:T(8,128)(2,1)}), bf16[16,24,3072]{2,1,0:T(8,128)(2,1)S(1)}, u32[]{:S(2)}, u32[]{:S(2)}) %all-to-all-start) | async-done | bytes 2359328 | tf_op jit(solution)/shard_map/while/body/eval_jaxpr/all_to_all | solution.py:11
  346.4 8.0 %all-to-all-start.1 = ((bf16[16,24,128]{2,1,0:T(8,128)(2,1)}), bf16[16,24,128]{2,1,0:T(8,128)(2,1)S(1)}, u32[]{:S(2)}, u32[]{:S(2)}) async-start(bf16[16,24,128]{2,1,0:T(8,128)(2,1)} %bitcast.121), calls=%async_computation.1 | async-start | bytes 196608 | tf_op jit(solution)/shard_map/while/body/eval_jaxpr/all_to_all | solution.py:121
  354.5 6.5 all-to-all-done.1
  382.2 25.4 %all-to-all-done = bf16[16,24,3072]{2,1,0:T(8,128)(2,1)S(1)} async-done(((bf16[16,24,3072]{2,1,0:T(8,128)(2,1)}), bf16[16,24,3072]{2,1,0:T(8,128)(2,1)S(1)}, u32[]{:S(2)}, u32[]{:S(2)}) %all-to-all-start) | async-done | bytes 2359328 | tf_op jit(solution)/shard_map/while/body/eval_jaxpr/all_to_all | solution.py:11
  413.2 8.0 %all-to-all-start.1 = ((bf16[16,24,128]{2,1,0:T(8,128)(2,1)}), bf16[16,24,128]{2,1,0:T(8,128)(2,1)S(1)}, u32[]{:S(2)}, u32[]{:S(2)}) async-start(bf16[16,24,128]{2,1,0:T(8,128)(2,1)} %bitcast.121), calls=%async_computation.1 | async-start | bytes 196608 | tf_op jit(solution)/shard_map/while/body/eval_jaxpr/all_to_all | solution.py:121
  449.0 25.4 %all-to-all-done = bf16[16,24,3072]{2,1,0:T(8,128)(2,1)S(1)} async-done(((bf16[16,24,3072]{2,1,0:T(8,128)(2,1)}), bf16[16,24,3072]{2,1,0:T(8,128)(2,1)S(1)}, u32[]{:S(2)}, u32[]{:S(2)}) %all-to-all-start) | async-done | bytes 2359328 | tf_op jit(solution)/shard_map/while/body/eval_jaxpr/all_to_all | solution.py:11
  480.0 8.0 %all-to-all-start.1 = ((bf16[16,24,128]{2,1,0:T(8,128)(2,1)}), bf16[16,24,128]{2,1,0:T(8,128)(2,1)S(1)}, u32[]{:S(2)}, u32[]{:S(2)}) async-start(bf16[16,24,128]{2,1,0:T(8,128)(2,1)} %bitcast.121), calls=%async_computation.1 | async-start | bytes 196608 | tf_op jit(solution)/shard_map/while/body/eval_jaxpr/all_to_all | solution.py:121
  488.1 6.5 all-to-all-done.1
  515.8 25.4 %all-to-all-done = bf16[16,24,3072]{2,1,0:T(8,128)(2,1)S(1)} async-done(((bf16[16,24,3072]{2,1,0:T(8,128)(2,1)}), bf16[16,24,3072]{2,1,0:T(8,128)(2,1)S(1)}, u32[]{:S(2)}, u32[]{:S(2)}) %all-to-all-start) | async-done | bytes 2359328 | tf_op jit(solution)/shard_map/while/body/eval_jaxpr/all_to_all | solution.py:11
  546.8 8.0 %all-to-all-start.1 = ((bf16[16,24,128]{2,1,0:T(8,128)(2,1)}), bf16[16,24,128]{2,1,0:T(8,128)(2,1)S(1)}, u32[]{:S(2)}, u32[]{:S(2)}) async-start(bf16[16,24,128]{2,1,0:T(8,128)(2,1)} %bitcast.121), calls=%async_computation.1 | async-start | bytes 196608 | tf_op jit(solution)/shard_map/while/body/eval_jaxpr/all_to_all | solution.py:121
  582.6 25.4 %all-to-all-done = bf16[16,24,3072]{2,1,0:T(8,128)(2,1)S(1)} async-done(((bf16[16,24,3072]{2,1,0:T(8,128)(2,1)}), bf16[16,24,3072]{2,1,0:T(8,128)(2,1)S(1)}, u32[]{:S(2)}, u32[]{:S(2)}) %all-to-all-start) | async-done | bytes 2359328 | tf_op jit(solution)/shard_map/while/body/eval_jaxpr/all_to_all | solution.py:11
  613.6 8.0 %all-to-all-start.1 = ((bf16[16,24,128]{2,1,0:T(8,128)(2,1)}), bf16[16,24,128]{2,1,0:T(8,128)(2,1)S(1)}, u32[]{:S(2)}, u32[]{:S(2)}) async-start(bf16[16,24,128]{2,1,0:T(8,128)(2,1)} %bitcast.121), calls=%async_computation.1 | async-start | bytes 196608 | tf_op jit(solution)/shard_map/while/body/eval_jaxpr/all_to_all | solution.py:121
  649.4 25.4 %all-to-all-done = bf16[16,24,3072]{2,1,0:T(8,128)(2,1)S(1)} async-done(((bf16[16,24,3072]{2,1,0:T(8,128)(2,1)}), bf16[16,24,3072]{2,1,0:T(8,128)(2,1)S(1)}, u32[]{:S(2)}, u32[]{:S(2)}) %all-to-all-start) | async-done | bytes 2359328 | tf_op jit(solution)/shard_map/while/body/eval_jaxpr/all_to_all | solution.py:11
  680.4 8.0 %all-to-all-start.1 = ((bf16[16,24,128]{2,1,0:T(8,128)(2,1)}), bf16[16,24,128]{2,1,0:T(8,128)(2,1)S(1)}, u32[]{:S(2)}, u32[]{:S(2)}) async-start(bf16[16,24,128]{2,1,0:T(8,128)(2,1)} %bitcast.121), calls=%async_computation.1 | async-start | bytes 196608 | tf_op jit(solution)/shard_map/while/body/eval_jaxpr/all_to_all | solution.py:121
  708.0 11.1 %all_to_all.88 = bf16[2,384,2,128]{3,2,0,1:T(2,128)(2,1)S(1)} all-to-all(bf16[2,384,2,128]{3,2,0,1:T(2,128)(2,1)S(1)} %copy.49), channel_id=1, replica_groups=mesh['pipe'=8,'seq'=16] {'seq'}, dimensions={1} | all-to-all | bytes 786432 | tf_op jit(solution)/shard_map/all_to_all | solution.py:139
  (358 shorter events, 301.4 us)
Async XLA Ops:
  7.2 94.8 %all-gather.3.cloned.1.call-start = ((), (), s32[]{:S(2)}) async-start(), calls=%async_computation.4 | async-start | bytes 13369344 | tf_op jit(solution)/shard_map/all_gather | solution.py:101
  12.6 14.8 %all-to-all-start.2 = ((bf16[16,2,3072]{2,1,0:T(2,128)(2,1)}), bf16[16,2,3072]{2,1,0:T(2,128)(2,1)S(1)}, u32[]{:S(2)}, u32[]{:S(2)}) async-start(bf16[16,2,3072]{2,1,0:T(2,128)(2,1)} %reshape.490), calls=%async_computation.2 | async-start | bytes 393216 | tf_op jit(solution)/shard_map/all_to_all | solution.py:100
  105.3 39.4 %all-to-all-start = ((bf16[16,24,3072]{2,1,0:T(8,128)(2,1)}), bf16[16,24,3072]{2,1,0:T(8,128)(2,1)S(1)}, u32[]{:S(2)}, u32[]{:S(2)}) async-start(bf16[16,24,3072]{2,1,0:T(8,128)(2,1)} %broadcast_in_dim.53), calls=%async_computation | async-start | bytes 4718592 | tf_op jit(solution)/shard_map/while/body/eval_jaxpr/all_to_all | solution.py:11
  150.2 10.3 %all-to-all-start.1 = ((bf16[16,24,128]{2,1,0:T(8,128)(2,1)}), bf16[16,24,128]{2,1,0:T(8,128)(2,1)S(1)}, u32[]{:S(2)}, u32[]{:S(2)}) async-start(bf16[16,24,128]{2,1,0:T(8,128)(2,1)} %bitcast.121), calls=%async_computation.1 | async-start | bytes 196608 | tf_op jit(solution)/shard_map/while/body/eval_jaxpr/all_to_all | solution.py:121
  175.8 31.2 %all-to-all-start = ((bf16[16,24,3072]{2,1,0:T(8,128)(2,1)}), bf16[16,24,3072]{2,1,0:T(8,128)(2,1)S(1)}, u32[]{:S(2)}, u32[]{:S(2)}) async-start(bf16[16,24,3072]{2,1,0:T(8,128)(2,1)} %broadcast_in_dim.53), calls=%async_computation | async-start | bytes 4718592 | tf_op jit(solution)/shard_map/while/body/eval_jaxpr/all_to_all | solution.py:11
  212.5 14.7 %all-to-all-start.1 = ((bf16[16,24,128]{2,1,0:T(8,128)(2,1)}), bf16[16,24,128]{2,1,0:T(8,128)(2,1)S(1)}, u32[]{:S(2)}, u32[]{:S(2)}) async-start(bf16[16,24,128]{2,1,0:T(8,128)(2,1)} %bitcast.121), calls=%async_computation.1 | async-start | bytes 196608 | tf_op jit(solution)/shard_map/while/body/eval_jaxpr/all_to_all | solution.py:121
  242.6 31.1 %all-to-all-start = ((bf16[16,24,3072]{2,1,0:T(8,128)(2,1)}), bf16[16,24,3072]{2,1,0:T(8,128)(2,1)S(1)}, u32[]{:S(2)}, u32[]{:S(2)}) async-start(bf16[16,24,3072]{2,1,0:T(8,128)(2,1)} %broadcast_in_dim.53), calls=%async_computation | async-start | bytes 4718592 | tf_op jit(solution)/shard_map/while/body/eval_jaxpr/all_to_all | solution.py:11
  279.3 14.6 %all-to-all-start.1 = ((bf16[16,24,128]{2,1,0:T(8,128)(2,1)}), bf16[16,24,128]{2,1,0:T(8,128)(2,1)S(1)}, u32[]{:S(2)}, u32[]{:S(2)}) async-start(bf16[16,24,128]{2,1,0:T(8,128)(2,1)} %bitcast.121), calls=%async_computation.1 | async-start | bytes 196608 | tf_op jit(solution)/shard_map/while/body/eval_jaxpr/all_to_all | solution.py:121
  300.2 6.2 collective-permute-start
  309.6 31.2 %all-to-all-start = ((bf16[16,24,3072]{2,1,0:T(8,128)(2,1)}), bf16[16,24,3072]{2,1,0:T(8,128)(2,1)S(1)}, u32[]{:S(2)}, u32[]{:S(2)}) async-start(bf16[16,24,3072]{2,1,0:T(8,128)(2,1)} %broadcast_in_dim.53), calls=%async_computation | async-start | bytes 4718592 | tf_op jit(solution)/shard_map/while/body/eval_jaxpr/all_to_all | solution.py:11
  346.4 14.7 %all-to-all-start.1 = ((bf16[16,24,128]{2,1,0:T(8,128)(2,1)}), bf16[16,24,128]{2,1,0:T(8,128)(2,1)S(1)}, u32[]{:S(2)}, u32[]{:S(2)}) async-start(bf16[16,24,128]{2,1,0:T(8,128)(2,1)} %bitcast.121), calls=%async_computation.1 | async-start | bytes 196608 | tf_op jit(solution)/shard_map/while/body/eval_jaxpr/all_to_all | solution.py:121
  367.4 5.9 collective-permute-start
  376.4 31.2 %all-to-all-start = ((bf16[16,24,3072]{2,1,0:T(8,128)(2,1)}), bf16[16,24,3072]{2,1,0:T(8,128)(2,1)S(1)}, u32[]{:S(2)}, u32[]{:S(2)}) async-start(bf16[16,24,3072]{2,1,0:T(8,128)(2,1)} %broadcast_in_dim.53), calls=%async_computation | async-start | bytes 4718592 | tf_op jit(solution)/shard_map/while/body/eval_jaxpr/all_to_all | solution.py:11
  413.2 14.7 %all-to-all-start.1 = ((bf16[16,24,128]{2,1,0:T(8,128)(2,1)}), bf16[16,24,128]{2,1,0:T(8,128)(2,1)S(1)}, u32[]{:S(2)}, u32[]{:S(2)}) async-start(bf16[16,24,128]{2,1,0:T(8,128)(2,1)} %bitcast.121), calls=%async_computation.1 | async-start | bytes 196608 | tf_op jit(solution)/shard_map/while/body/eval_jaxpr/all_to_all | solution.py:121
  443.2 31.2 %all-to-all-start = ((bf16[16,24,3072]{2,1,0:T(8,128)(2,1)}), bf16[16,24,3072]{2,1,0:T(8,128)(2,1)S(1)}, u32[]{:S(2)}, u32[]{:S(2)}) async-start(bf16[16,24,3072]{2,1,0:T(8,128)(2,1)} %broadcast_in_dim.53), calls=%async_computation | async-start | bytes 4718592 | tf_op jit(solution)/shard_map/while/body/eval_jaxpr/all_to_all | solution.py:11
  480.0 14.7 %all-to-all-start.1 = ((bf16[16,24,128]{2,1,0:T(8,128)(2,1)}), bf16[16,24,128]{2,1,0:T(8,128)(2,1)S(1)}, u32[]{:S(2)}, u32[]{:S(2)}) async-start(bf16[16,24,128]{2,1,0:T(8,128)(2,1)} %bitcast.121), calls=%async_computation.1 | async-start | bytes 196608 | tf_op jit(solution)/shard_map/while/body/eval_jaxpr/all_to_all | solution.py:121
  501.0 5.9 collective-permute-start
  510.0 31.2 %all-to-all-start = ((bf16[16,24,3072]{2,1,0:T(8,128)(2,1)}), bf16[16,24,3072]{2,1,0:T(8,128)(2,1)S(1)}, u32[]{:S(2)}, u32[]{:S(2)}) async-start(bf16[16,24,3072]{2,1,0:T(8,128)(2,1)} %broadcast_in_dim.53), calls=%async_computation | async-start | bytes 4718592 | tf_op jit(solution)/shard_map/while/body/eval_jaxpr/all_to_all | solution.py:11
  546.8 14.7 %all-to-all-start.1 = ((bf16[16,24,128]{2,1,0:T(8,128)(2,1)}), bf16[16,24,128]{2,1,0:T(8,128)(2,1)S(1)}, u32[]{:S(2)}, u32[]{:S(2)}) async-start(bf16[16,24,128]{2,1,0:T(8,128)(2,1)} %bitcast.121), calls=%async_computation.1 | async-start | bytes 196608 | tf_op jit(solution)/shard_map/while/body/eval_jaxpr/all_to_all | solution.py:121
  576.8 31.2 %all-to-all-start = ((bf16[16,24,3072]{2,1,0:T(8,128)(2,1)}), bf16[16,24,3072]{2,1,0:T(8,128)(2,1)S(1)}, u32[]{:S(2)}, u32[]{:S(2)}) async-start(bf16[16,24,3072]{2,1,0:T(8,128)(2,1)} %broadcast_in_dim.53), calls=%async_computation | async-start | bytes 4718592 | tf_op jit(solution)/shard_map/while/body/eval_jaxpr/all_to_all | solution.py:11
  613.6 14.7 %all-to-all-start.1 = ((bf16[16,24,128]{2,1,0:T(8,128)(2,1)}), bf16[16,24,128]{2,1,0:T(8,128)(2,1)S(1)}, u32[]{:S(2)}, u32[]{:S(2)}) async-start(bf16[16,24,128]{2,1,0:T(8,128)(2,1)} %bitcast.121), calls=%async_computation.1 | async-start | bytes 196608 | tf_op jit(solution)/shard_map/while/body/eval_jaxpr/all_to_all | solution.py:121
  634.6 5.9 collective-permute-start
  643.6 31.2 %all-to-all-start = ((bf16[16,24,3072]{2,1,0:T(8,128)(2,1)}), bf16[16,24,3072]{2,1,0:T(8,128)(2,1)S(1)}, u32[]{:S(2)}, u32[]{:S(2)}) async-start(bf16[16,24,3072]{2,1,0:T(8,128)(2,1)} %broadcast_in_dim.53), calls=%async_computation | async-start | bytes 4718592 | tf_op jit(solution)/shard_map/while/body/eval_jaxpr/all_to_all | solution.py:11
  680.4 14.7 %all-to-all-start.1 = ((bf16[16,24,128]{2,1,0:T(8,128)(2,1)}), bf16[16,24,128]{2,1,0:T(8,128)(2,1)S(1)}, u32[]{:S(2)}, u32[]{:S(2)}) async-start(bf16[16,24,128]{2,1,0:T(8,128)(2,1)} %bitcast.121), calls=%async_computation.1 | async-start | bytes 196608 | tf_op jit(solution)/shard_map/while/body/eval_jaxpr/all_to_all | solution.py:121
  (45 other events, 530.3 us)
Sparse Core Ops, SparseCore 0:
  10.1 91.8 all-gather.2
where the time goes:
time: 741 us; the launch traced here: 727 us
  waiting for transfers between devices  410 us (55%)
  starting transfers between devices  121 us (16%)
  matrix products  95.4 us (13%)
  local copies, waits for them, and re-layouts  51.1 us (7%)
  other arithmetic  22.6 us (3%)
  between operations  14.2 us (2%)
  blocking collectives  11.1 us (1%)
    all_to_all x9, waiting for transfers between devices, from_everyone(): return lax.all_to_all(copies, axis, split_axis=0, concat_axis=0, tiled=True)  235 us
    all_gather x1, waiting for transfers between devices, body(): out_full = lax.all_gather(output_proj[0], 'seq', axis=0, tiled=True)  72.3 us
    all_to_all x9, starting transfers between devices, turn_step(): lax.all_to_all(attended, 'seq', split_axis=0, concat_axis=1, tiled=True)  67.4 us
    all_to_all x9, waiting for transfers between devices, turn_step(): lax.all_to_all(attended, 'seq', split_axis=0, concat_axis=1, tiled=True)  58.7 us
    dot_general x9, matrix products, turn_step(): update = jnp.dot(regrouped, out_full, preferred_element_type=jnp.float32)  57.3 us
    ppermute x9, waiting for transfers between devices, shifted(): lax.ppermute(value, axis, [(source, source + steps) for source in range(f...  40.8 us
    all_to_all x9, starting transfers between devices, from_everyone(): return lax.all_to_all(copies, axis, split_axis=0, concat_axis=0, tiled=True)  34.8 us
    dot_general x9, matrix products, project(): return jnp.dot(block_rows, weight_flat, preferred_element_type=jnp.float32)  27.8 us
  transfers between devices with their start and end apart: 29, of which 29 were waited for; matrix products, arithmetic and copies ran while one was open for 4% of the time, Pallas kernels for 0%

commit v1 on v0

v1 whole, which is shorter than its diff:
```python
import functools
import math

import jax
import jax.numpy as jnp
from jax import lax
from jax.experimental import pallas as pl
from jax.experimental.pallas import tpu as pltpu
from jax.sharding import PartitionSpec as P

MESH = pl.DeviceIdType.MESH
SIDE = 4


def block_kernel(
    hid, shift, scale, gate, gain, w, o, st, bo_out, fc_out,
    xp, nga, ngb, xr, sg, kv, qb, og, att, atg, xo, bob, fcs, fcb,
    s_st, r_st, s_o, r_o, s_xp, r_xp, s_xr, r_xr, s_1a, r_1a, s_1b, r_1b,
    s_2a, r_2a, s_2b, r_2b, s_at, r_at, s_fc, r_fc, s_bo, r_bo,
):
    l = lax.axis_index("pipe")
    h = lax.axis_index("seq")
    sections = lax.axis_size("pipe")
    count = lax.axis_size("seq")
    i = lax.div(h, SIDE)
    j = lax.rem(h, SIDE)
    half = w.shape[0] // 2
    rows, piece = hid.shape[2], hid.shape[3]
    group = SIDE * rows
    hs = gain.shape[1]
    factor = 1.0 / math.sqrt(hs)
    nxt = lax.rem(l + 1, sections)
    prv = lax.rem(l + sections - 1, sections)

    def send(src, dst, ssem, rsem, pipe, seq):
        pltpu.make_async_remote_copy(
            src_ref=src, dst_ref=dst, send_sem=ssem, recv_sem=rsem,
            device_id=(pipe, seq), device_id_type=MESH,
        ).start()

    def local(src, dst, sem):
        pltpu.make_async_copy(src, dst, sem).start()

    def await_bytes(region, sem):
        pltpu.make_async_copy(region, region, sem).wait()

    def other(k):
        return lax.rem(h + k, count)

    barrier = pltpu.get_barrier_semaphore()
    for k in range(1, SIDE * SIDE):
        pl.semaphore_signal(barrier, inc=1, device_id=(l, other(k)), device_id_type=MESH)
    for k in range(SIDE):
        pl.semaphore_signal(barrier, inc=1, device_id=(nxt, SIDE * i + k), device_id_type=MESH)
        pl.semaphore_signal(barrier, inc=1, device_id=(prv, SIDE * i + k), device_id_type=MESH)

    @pl.when(l == 0)
    def _():
        for p in range(2):
            local(hid.at[p], xp.at[p], r_xp.at[p])

    pl.semaphore_wait(barrier, SIDE * SIDE - 1 + 2 * SIDE)

    def send_out_proj():
        for k in range(1, SIDE * SIDE):
            t = other(k)
            col = pl.multiple_of(lax.rem(t, SIDE) * piece, 128)
            send(o.at[:, pl.ds(col, piece)], og.at[h], s_o, r_o, l, t)
        col = pl.multiple_of(j * piece, 128)
        local(o.at[:, pl.ds(col, piece)], og.at[h], r_o)

    def send_stale():
        for k in range(1, SIDE * SIDE):
            t = other(k)
            send(st.at[t], sg.at[h], s_st, r_st, l, t)
        local(st.at[h], sg.at[h], r_st)

    @pl.when(l > 0)
    def _():
        send_stale()
        send_out_proj()

    def patch(p, carry):
        await_bytes(xp.at[p], r_xp.at[p])
        x = xp[p].astype(jnp.float32)
        width = SIDE * piece
        mean = jnp.sum(jnp.sum(x, axis=0), axis=-1, keepdims=True) / width
        cen = x - mean[None]
        spread = jnp.sum(jnp.sum(cen * cen, axis=0), axis=-1, keepdims=True) / width
        inv = 1.0 / jnp.sqrt(spread + 1e-06)
        normed = (cen * inv[None] * (1.0 + scale[...]) + shift[...]).astype(jnp.bfloat16)
        nga[p, i, j, :, :piece] = normed[0]
        nga[p, i, j, :, piece:] = normed[1]
        ngb[p, j, i, :, :piece] = normed[2]
        ngb[p, j, i, :, piece:] = normed[3]
        for k in (2, 1, 3):
            jj = lax.rem(j + k, SIDE)
            ii = lax.rem(i + k, SIDE)
            send(nga.at[p, i, j], nga.at[p, i, j], s_1a.at[p], r_1a.at[p], l, SIDE * i + jj)
            send(ngb.at[p, j, i], ngb.at[p, j, i], s_1b.at[p], r_1b.at[p], l, SIDE * ii + j)
        await_bytes(nga.at[p, 0, pl.ds(0, SIDE - 1)], r_1a.at[p])
        for k in (2, 1, 3):
            ii = lax.rem(i + k, SIDE)
            send(nga.at[p, i], nga.at[p, i], s_2a.at[p], r_2a.at[p], l, SIDE * ii + j)
        await_bytes(ngb.at[p, 0, pl.ds(0, SIDE - 1)], r_1b.at[p])
        for k in (2, 1, 3):
            jj = lax.rem(j + k, SIDE)
            send(ngb.at[p, j], ngb.at[p, j], s_2b.at[p], r_2b.at[p], l, SIDE * i + jj)
        for k in range(1, SIDE):
            jj = lax.rem(j + k, SIDE)
            send(xp.at[p, jj], xr.at[p, j], s_xr.at[p], r_xr.at[p], l, SIDE * i + jj)
        local(xp.at[p, j], xr.at[p, j], r_xr.at[p])

        @pl.when((l == 0) & (p == 0))
        def _():
            send_stale()
            send_out_proj()

        @pl.when(p == 0)
        def _():
            await_bytes(sg, r_st)
            for c in range(2):
                old = sg[:, c].astype(jnp.float32).reshape(count * rows, hs)
                kv[0, c] = old.astype(jnp.bfloat16)

        await_bytes(nga.at[p, pl.ds(0, SIDE - 1)], r_2a.at[p])
        await_bytes(ngb.at[p, pl.ds(0, SIDE - 1)], r_2b.at[p])

        def project(g, c):
            left = jnp.concatenate([nga[p, g, m].astype(jnp.float32) for m in range(SIDE)], axis=0)
            right = jnp.concatenate([ngb[p, m, g].astype(jnp.float32) for m in range(SIDE)], axis=0)
            out = jnp.dot(
                left.astype(jnp.bfloat16), w[:half], preferred_element_type=jnp.float32
            ) + jnp.dot(right.astype(jnp.bfloat16), w[half:], preferred_element_type=jnp.float32)
            for c in range(2):
                part = out[:, c * hs : (c + 1) * hs]
                square = jnp.mean(part * part, axis=-1, keepdims=True)
                part = part * (1.0 / jnp.sqrt(square + 1e-06)) * gain[c : c + 1, :]
                if c == 0:
                    qb[g] = part.astype(jnp.bfloat16)
                else:
                    keys = part
            values = out[:, 2 * hs :]
            kv[p + 1, 0, pl.ds(pl.multiple_of(g * group, group), group)] = keys.astype(jnp.bfloat16)
            kv[p + 1, 1, pl.ds(pl.multiple_of(g * group, group), group)] = values.astype(jnp.bfloat16)
            fcs[p, pl.ds(g * SIDE, SIDE), 0] = keys.reshape(SIDE, rows, hs).astype(jnp.bfloat16)
            fcs[p, pl.ds(g * SIDE, SIDE), 1] = values.reshape(SIDE, rows, hs).astype(jnp.bfloat16)
            return c

        lax.fori_loop(0, SIDE, project, 0)

        def attend(g):
            q = qb[g]
            dims = (((1,), (1,)), ((), ()))
            near = lax.dot_general(q, kv[p + 1, 0], dims, preferred_element_type=jnp.float32)
            far = lax.dot_general(q, kv[p, 0], dims, preferred_element_type=jnp.float32)
            near = jnp.exp(near * factor)
            far = jnp.exp(far * factor)
            den = jnp.sum(near, axis=-1, keepdims=True) + jnp.sum(far, axis=-1, keepdims=True)
            inv = 1.0 / den
            near = (near * inv).astype(jnp.bfloat16)
            far = (far * inv).astype(jnp.bfloat16)
            mixed = jnp.dot(near, kv[p + 1, 1], preferred_element_type=jnp.float32)
            mixed = mixed + jnp.dot(far, kv[p, 1], preferred_element_type=jnp.float32)
            att[p, g] = mixed.astype(jnp.bfloat16)

        for gg in (2, 1, 3, 0):
            g = lax.rem(i + gg, SIDE)
            attend(g)
            for k in range(1 if gg == 0 else 0, SIDE):
                jj = lax.rem(j + k, SIDE)
                send(att.at[p, g], atg.at[p, h], s_at.at[p], r_at.at[p], l, SIDE * g + jj)
        local(att.at[p, i], atg.at[p, h], r_at.at[p])

        for k in range(1, SIDE * SIDE):
            t = other(k)
            send(fcs.at[p, t], fcb.at[p, h], s_fc.at[p], r_fc.at[p], l, t)
        local(fcs.at[p, h], fcb.at[p, h], r_fc.at[p])

        @pl.when(p == 0)
        def _():
            await_bytes(og, r_o)

        await_bytes(xr.at[p], r_xr.at[p])
        base = xr[p].astype(jnp.float32).reshape(group, piece)
        await_bytes(atg.at[p], r_at.at[p])
        mixed = jnp.concatenate([atg[p, m] for m in range(SIDE * SIDE)], axis=1)
        update = jnp.dot(
            mixed, og[...].reshape(SIDE * SIDE * hs, piece), preferred_element_type=jnp.float32
        )
        result = base + gate[j] * update
        xo[p] = result.reshape(SIDE, rows, piece).astype(jnp.bfloat16)

        @pl.when(l < sections - 1)
        def _():
            for k in range(SIDE):
                send(xo.at[p, k], xp.at[p, j], s_xp.at[p], r_xp.at[p], nxt, SIDE * i + k)

        for k in range(1, SIDE):
            kk = lax.rem(j + k, SIDE)
            send(xo.at[p, kk], bob.at[p, j], s_bo.at[p], r_bo.at[p], l, SIDE * i + kk)
        local(xo.at[p, j], bob.at[p, j], r_bo.at[p])
        return carry

    lax.fori_loop(0, 2, patch, 0)

    for p in range(2):
        await_bytes(fcb.at[p], r_fc.at[p])
        await_bytes(bob.at[p], r_bo.at[p])
    fc_out[...] = fcb[...]
    bo_out[...] = bob[...]
    most = pl.ds(0, SIDE * SIDE - 1)
    three = pl.ds(0, SIDE - 1)
    await_bytes(sg.at[most], s_st)
    await_bytes(og.at[most], s_o)
    for p in range(2):
        await_bytes(nga.at[p, 0, three], s_1a.at[p])
        await_bytes(ngb.at[p, 0, three], s_1b.at[p])
        await_bytes(nga.at[p, three], s_2a.at[p])
        await_bytes(ngb.at[p, three], s_2b.at[p])
        await_bytes(xr.at[p, three], s_xr.at[p])
        await_bytes(atg.at[p, most], s_at.at[p])
        await_bytes(fcb.at[p, most], s_fc.at[p])
        await_bytes(bob.at[p, three], s_bo.at[p])

    @pl.when(l < sections - 1)
    def _():
        for p in range(2):
            await_bytes(xp.at[p], s_xp.at[p])


def body(hidden, mod_shift, mod_scale, mod_gate, norm_gain, input_proj, output_proj, stale_cache):
    patches, rows, width = hidden.shape
    hs = norm_gain.shape[2]
    count = SIDE * SIDE
    piece = width // SIDE
    half = width // 2
    bf, f32 = jnp.bfloat16, jnp.float32
    hid = hidden.reshape(patches, rows, SIDE, piece).transpose(0, 2, 1, 3)
    shift = mod_shift.reshape(SIDE, 1, piece)
    scale = mod_scale.reshape(SIDE, 1, piece)
    gate = mod_gate.reshape(SIDE, 1, piece)
    w = input_proj[0].reshape(width, 3 * hs)
    st = stale_cache[0, 1].reshape(rows, 2, count, hs).transpose(2, 1, 0, 3)
    vmem = pl.BlockSpec(memory_space=pltpu.VMEM)
    one = pltpu.SemaphoreType.DMA
    pair = pltpu.SemaphoreType.DMA((2,))
    bo, fc = pl.pallas_call(
        block_kernel,
        out_shape=(
            jax.ShapeDtypeStruct((patches, SIDE, rows, piece), bf),
            jax.ShapeDtypeStruct((patches, count, 2, rows, hs), bf),
        ),
        in_specs=[vmem] * 8,
        out_specs=(vmem, vmem),
        scratch_shapes=[
            pltpu.VMEM((patches, SIDE, rows, piece), bf),
            pltpu.VMEM((patches, SIDE, SIDE, rows, half), bf),
            pltpu.VMEM((patches, SIDE, SIDE, rows, half), bf),
            pltpu.VMEM((patches, SIDE, rows, piece), bf),
            pltpu.VMEM((count, 2, rows, hs), bf),
            pltpu.VMEM((patches + 1, 2, count * rows, hs), bf),
            pltpu.VMEM((SIDE, SIDE * rows, hs), bf),
            pltpu.VMEM((count, hs, piece), bf),
            pltpu.VMEM((patches, SIDE, SIDE * rows, hs), bf),
            pltpu.VMEM((patches, count, SIDE * rows, hs), bf),
            pltpu.VMEM((patches, SIDE, rows, piece), bf),
            pltpu.VMEM((patches, SIDE, rows, piece), bf),
            pltpu.VMEM((patches, count, 2, rows, hs), bf),
            pltpu.VMEM((patches, count, 2, rows, hs), bf),
            one, one, one, one,
        ] + [pair] * 18,
        compiler_params=pltpu.CompilerParams(
            collective_id=0, has_side_effects=True, vmem_limit_bytes=56 * 1024 * 1024
        ),
    )(hid, shift, scale, gate, norm_gain[0], w, output_proj[0], st)
    outputs = bo.transpose(0, 2, 1, 3).reshape(1, patches, rows, width)
    cache = fc.transpose(0, 3, 2, 1, 4).reshape(1, patches, rows, 2, count * hs)
    return outputs, cache


def solution(mesh):
    in_specs = (
        P(None, "seq", None),
        P("pipe", None),
        P("pipe", None),
        P("pipe", None),
        P("pipe", None, None),
        P("pipe", None, None, "seq"),
        P("pipe", "seq", None),
        P("pipe", None, "seq", None, None),
    )
    out_specs = (P("pipe", None, "seq", None), P("pipe", None, "seq", None, None))
    return jax.shard_map(body, mesh=mesh, in_specs=in_specs, out_specs=out_specs, check_vma=False)
```

time: 741 us -> 329 us (0.44); the launches traced: 727 us -> 329 us
  waiting for transfers between devices: 410 us -> 0 us
  Pallas kernels: 0 us -> 317 us
  starting transfers between devices: 121 us -> 0 us
  matrix products: 95.4 us -> 0 us
  local copies, waits for them, and re-layouts: 51.1 us -> 10.9 us
  other arithmetic: 22.6 us -> 0 us
  between operations: 14.2 us -> 0.67 us
  blocking collectives: 11.1 us -> 0 us
    pallas_call x0 -> x1, Pallas kernels: none -> 317 us  [body(): pl.pallas_call(block_kernel, out_shape=(jax.ShapeDtypeStruct((patches, SI...]
    all_to_all x19 -> x0, waiting for transfers between devices: 296 us -> none  [the longest x9 235 us: from_everyone(): return lax.all_to_all(copies, axis, split_axis=0, concat_axis=0, tiled=True)]
    all_to_all x19 -> x0, starting transfers between devices: 110 us -> none  [the longest x9 67.4 us: turn_step(): lax.all_to_all(attended, 'seq', split_axis=0, concat_axis=1, tiled=True)]
    dot_general x54 -> x0, matrix products: 95.4 us -> none  [the longest x9 57.3 us: turn_step(): update = jnp.dot(regrouped, out_full, preferred_element_type=jnp.float32)]
    all_gather x1 -> x0, waiting for transfers between devices: 72.3 us -> none  [body(): out_full = lax.all_gather(output_proj[0], 'seq', axis=0, tiled=True)]
    ppermute x9 -> x0, waiting for transfers between devices: 40.8 us -> none  [shifted(): lax.ppermute(value, axis, [(source, source + steps) for source in range(f...]
    broadcast_in_dim x12 -> x0, local copies, waits for them, and re-layouts: 15.1 us -> none  [the longest x9 15 us: from_everyone(): copies = jnp.broadcast_to(array, (lax.axis_size(axis), *array.shape))]
    reduce_sum x27 -> x0, other arithmetic: 12 us -> none  [the longest x9 9.58 us: layer_norm(): centered = widened - jnp.mean(widened, axis=-1, keepdims=True)]
  transfers between devices with their start and end apart: 29 -> 0, of which waited for: 29 -> 0; matrix products, arithmetic and copies ran while one was open for 4% -> 0% of each run, Pallas kernels for 0% -> 0%
where the time goes in v1:
time: 329 us
  Pallas kernels  317 us (96%)
  local copies, waits for them, and re-layouts  10.9 us (3%)
    pallas_call x1, Pallas kernels, body(): pl.pallas_call(block_kernel, out_shape=(jax.ShapeDtypeStruct((patches, SI...  317 us

profile of v1, /device:TPU:25, one launch (start us, length us, event | category | flops | bytes accessed | tf_op | source)
XLA Modules:
  0.0 328.6 jit_solution(6463073166652552402)
XLA Ops:
  0.6 2.8 copy.12
  3.5 0.0 slice-start
  3.5 0.0 copy-start
  3.5 2.5 copy.15.w
  6.0 0.0 slice-done
  6.0 0.1 reshape.28
  6.1 0.8 copy.27
  6.9 0.0 copy-done
  6.9 0.7 copy.26
  7.6 317.0 %shard_map.95 = (bf16[2,4,24,768]{3,2,1,0:T(8,128)(2,1)}, bf16[2,16,2,24,128]{4,3,2,1,0:T(8,128)(2,1)}) custom-call(bf16[2,4,24,768]{3,2,1,0:T(8,128)(2,1)} %bitcast.21, f32[4,1,768]{2,1,0:T(1,128)} %bitcast.27, f32[4,1,768]{2,1,0:T(1,128)} %bitcast.28, f32[4,1,768]{2,1,0:T(1,128)} %bitcast.29, f32[2,128]{1,0:T(2,128)} %bitcast.30, ...), custom_call_target="tpu_custom_call" | custom-call | tf_op jit(solution)/shard_map/pallas_call | solution.py:248
  324.7 1.1 copy.21
  325.8 0.8 reshape.29
  326.6 1.1 copy.16
  327.7 0.9 reshape.26
Async XLA Ops:
  3.5 2.5 slice-start
  3.5 3.4 %copy-start = (bf16[2,24,3072]{2,1,0:T(8,128)(2,1)S(1)}, bf16[2,24,3072]{2,1,0:T(8,128)(2,1)}, u32[]{:S(2)}) copy-start(bf16[2,24,3072]{2,1,0:T(8,128)(2,1)} %param.8) | copy-start | bytes 884740

commit v2 on v1

--- a/solution.py
+++ b/solution.py
@@ -13,10 +13,10 @@
 
 
 def block_kernel(
-    hid, shift, scale, gate, gain, w, o, st, bo_out, fc_out,
+    hid, shift, scale, gate, gain, w_hbm, o, st, bo_out, fc_out,
     xp, nga, ngb, xr, sg, kv, qb, og, att, atg, xo, bob, fcs, fcb,
     s_st, r_st, s_o, r_o, s_xp, r_xp, s_xr, r_xr, s_1a, r_1a, s_1b, r_1b,
-    s_2a, r_2a, s_2b, r_2b, s_at, r_at, s_fc, r_fc, s_bo, r_bo,
+    s_2a, r_2a, s_2b, r_2b, s_at, r_at, s_fc, r_fc, s_bo, r_bo, w, s_w, go,
 ):
     l = lax.axis_index("pipe")
     h = lax.axis_index("seq")
@@ -24,13 +24,17 @@
     count = lax.axis_size("seq")
     i = lax.div(h, SIDE)
     j = lax.rem(h, SIDE)
-    half = w.shape[0] // 2
-    rows, piece = hid.shape[2], hid.shape[3]
+    half = w.shape[1] // 2
+    rows, piece = xp.shape[2], xp.shape[3]
     group = SIDE * rows
     hs = gain.shape[1]
     factor = 1.0 / math.sqrt(hs)
     nxt = lax.rem(l + 1, sections)
     prv = lax.rem(l + sections - 1, sections)
+    even = lax.rem(l, 2) == 0
+    partner = l + 1 - 2 * lax.rem(l, 2)
+    load_w = pltpu.make_async_copy(w_hbm, w, s_w)
+    load_w.start()
 
     def send(src, dst, ssem, rsem, pipe, seq):
         pltpu.make_async_remote_copy(
@@ -57,17 +61,22 @@
     @pl.when(l == 0)
     def _():
         for p in range(2):
-            local(hid.at[p], xp.at[p], r_xp.at[p])
+            for q in range(SIDE):
+                local(hid.at[p, :, pl.ds(q * piece, piece)], xp.at[p, q], r_xp.at[p])
 
     pl.semaphore_wait(barrier, SIDE * SIDE - 1 + 2 * SIDE)
 
-    def send_out_proj():
-        for k in range(1, SIDE * SIDE):
+    def send_out_proj(first, last):
+        for k in range(max(first, 1), last):
             t = other(k)
             col = pl.multiple_of(lax.rem(t, SIDE) * piece, 128)
             send(o.at[:, pl.ds(col, piece)], og.at[h], s_o, r_o, l, t)
-        col = pl.multiple_of(j * piece, 128)
-        local(o.at[:, pl.ds(col, piece)], og.at[h], r_o)
+        if first == 0:
+            col = pl.multiple_of(j * piece, 128)
+            local(o.at[:, pl.ds(col, piece)], og.at[h], r_o)
+
+    def tell_partner():
+        pl.semaphore_signal(go, inc=1, device_id=(partner, h), device_id_type=MESH)
 
     def send_stale():
         for k in range(1, SIDE * SIDE):
@@ -75,10 +84,22 @@
             send(st.at[t], sg.at[h], s_st, r_st, l, t)
         local(st.at[h], sg.at[h], r_st)
 
+    everyone = SIDE * SIDE
+
     @pl.when(l > 0)
     def _():
         send_stale()
-        send_out_proj()
+
+    @pl.when((l > 0) & even)
+    def _():
+        send_out_proj(0, everyone)
+        await_bytes(og, r_o)
+        tell_partner()
+
+    @pl.when(lax.rem(l, 2) == 1)
+    def _():
+        pl.semaphore_wait(go, 1)
+        send_out_proj(0, everyone // 2)
 
     def patch(p, carry):
         await_bytes(xp.at[p], r_xp.at[p])
@@ -93,6 +114,10 @@
         nga[p, i, j, :, piece:] = normed[1]
         ngb[p, j, i, :, :piece] = normed[2]
         ngb[p, j, i, :, piece:] = normed[3]
+        @pl.when((p == 1) & even)
+        def _():
+            pl.semaphore_wait(go, 1)
+
         for k in (2, 1, 3):
             jj = lax.rem(j + k, SIDE)
             ii = lax.rem(i + k, SIDE)
@@ -114,10 +139,15 @@
         @pl.when((l == 0) & (p == 0))
         def _():
             send_stale()
-            send_out_proj()
+            send_out_proj(0, everyone)
+
+        @pl.when((lax.rem(l, 2) == 1) & (p == 0))
+        def _():
+            send_out_proj(everyone // 2, everyone)
 
         @pl.when(p == 0)
         def _():
+            load_w.wait()
             await_bytes(sg, r_st)
             for c in range(2):
                 old = sg[:, c].astype(jnp.float32).reshape(count * rows, hs)
@@ -126,12 +156,18 @@
         await_bytes(nga.at[p, pl.ds(0, SIDE - 1)], r_2a.at[p])
         await_bytes(ngb.at[p, pl.ds(0, SIDE - 1)], r_2b.at[p])
 
+        @pl.when((p == 0) & (lax.rem(l, 2) == 1))
+        def _():
+            tell_partner()
+
         def project(g, c):
             left = jnp.concatenate([nga[p, g, m].astype(jnp.float32) for m in range(SIDE)], axis=0)
             right = jnp.concatenate([ngb[p, m, g].astype(jnp.float32) for m in range(SIDE)], axis=0)
+            first = jnp.concatenate([w[m, :half] for m in range(3)], axis=1)
+            second = jnp.concatenate([w[m, half:] for m in range(3)], axis=1)
             out = jnp.dot(
-                left.astype(jnp.bfloat16), w[:half], preferred_element_type=jnp.float32
-            ) + jnp.dot(right.astype(jnp.bfloat16), w[half:], preferred_element_type=jnp.float32)
+                left.astype(jnp.bfloat16), first, preferred_element_type=jnp.float32
+            ) + jnp.dot(right.astype(jnp.bfloat16), second, preferred_element_type=jnp.float32)
             for c in range(2):
                 part = out[:, c * hs : (c + 1) * hs]
                 square = jnp.mean(part * part, axis=-1, keepdims=True)
@@ -177,9 +213,13 @@
             send(fcs.at[p, t], fcb.at[p, h], s_fc.at[p], r_fc.at[p], l, t)
         local(fcs.at[p, h], fcb.at[p, h], r_fc.at[p])
 
-        @pl.when(p == 0)
+        @pl.when((p == 0) & ((l == 0) | (lax.rem(l, 2) == 1)))
         def _():
             await_bytes(og, r_o)
+
+        @pl.when((p == 0) & (l == 0))
+        def _():
+            tell_partner()
 
         await_bytes(xr.at[p], r_xr.at[p])
         base = xr[p].astype(jnp.float32).reshape(group, piece)
@@ -208,7 +248,9 @@
         await_bytes(fcb.at[p], r_fc.at[p])
         await_bytes(bob.at[p], r_bo.at[p])
     fc_out[...] = fcb[...]
-    bo_out[...] = bob[...]
+    for p in range(2):
+        for q in range(SIDE):
+            bo_out[p, :, q * piece : (q + 1) * piece] = bob[p, q]
     most = pl.ds(0, SIDE * SIDE - 1)
     three = pl.ds(0, SIDE - 1)
     await_bytes(sg.at[most], s_st)
@@ -236,22 +278,22 @@
     piece = width // SIDE
     half = width // 2
     bf, f32 = jnp.bfloat16, jnp.float32
-    hid = hidden.reshape(patches, rows, SIDE, piece).transpose(0, 2, 1, 3)
     shift = mod_shift.reshape(SIDE, 1, piece)
     scale = mod_scale.reshape(SIDE, 1, piece)
     gate = mod_gate.reshape(SIDE, 1, piece)
-    w = input_proj[0].reshape(width, 3 * hs)
+    w = input_proj[0].transpose(1, 0, 2)
     st = stale_cache[0, 1].reshape(rows, 2, count, hs).transpose(2, 1, 0, 3)
     vmem = pl.BlockSpec(memory_space=pltpu.VMEM)
+    hbm = pl.BlockSpec(memory_space=pl.ANY)
     one = pltpu.SemaphoreType.DMA
     pair = pltpu.SemaphoreType.DMA((2,))
     bo, fc = pl.pallas_call(
         block_kernel,
         out_shape=(
-            jax.ShapeDtypeStruct((patches, SIDE, rows, piece), bf),
+            jax.ShapeDtypeStruct((patches, rows, width), bf),
             jax.ShapeDtypeStruct((patches, count, 2, rows, hs), bf),
         ),
-        in_specs=[vmem] * 8,
+        in_specs=[vmem] * 5 + [hbm, hbm, vmem],
         out_specs=(vmem, vmem),
         scratch_shapes=[
             pltpu.VMEM((patches, SIDE, rows, piece), bf),
@@ -269,12 +311,16 @@
             pltpu.VMEM((patches, count, 2, rows, hs), bf),
             pltpu.VMEM((patches, count, 2, rows, hs), bf),
             one, one, one, one,
-        ] + [pair] * 18,
+        ] + [pair] * 18 + [
+            pltpu.VMEM((3, width, hs), bf),
+            one,
+            pltpu.SemaphoreType.REGULAR,
+        ],
         compiler_params=pltpu.CompilerParams(
             collective_id=0, has_side_effects=True, vmem_limit_bytes=56 * 1024 * 1024
         ),
-    )(hid, shift, scale, gate, norm_gain[0], w, output_proj[0], st)
-    outputs = bo.transpose(0, 2, 1, 3).reshape(1, patches, rows, width)
+    )(hidden, shift, scale, gate, norm_gain[0], w, output_proj[0], st)
+    outputs = bo[None]
     cache = fc.transpose(0, 3, 2, 1, 4).reshape(1, patches, rows, 2, count * hs)
     return outputs, cache
 

time: 329 us -> 357 us (1.085)
  Pallas kernels: 317 us -> 351 us
  local copies, waits for them, and re-layouts: 10.9 us -> 5.58 us
    pallas_call x1, Pallas kernels: 317 us -> 351 us  [body(): pl.pallas_call(block_kernel, out_shape=(jax.ShapeDtypeStruct((patches, ro...]
where the time goes in v2:
time: 357 us
  Pallas kernels  351 us (98%)
  local copies, waits for them, and re-layouts  5.58 us (2%)
    pallas_call x1, Pallas kernels, body(): pl.pallas_call(block_kernel, out_shape=(jax.ShapeDtypeStruct((patches, ro...  351 us

profile of v2, /device:TPU:25, one launch (start us, length us, event | category | flops | bytes accessed | tf_op | source)
XLA Modules:
  0.0 356.8 jit_solution(11907231585705990097)
XLA Ops:
  0.6 1.1 slice.3
  1.7 0.1 reshape.20
  1.8 0.8 copy.19
  2.6 350.5 %shard_map.95 = (bf16[2,24,3072]{2,1,0:T(8,128)(2,1)}, bf16[2,16,2,24,128]{4,3,2,1,0:T(8,128)(2,1)}) custom-call(bf16[2,24,3072]{2,1,0:T(8,128)(2,1)} %hid.1, f32[4,1,768]{2,1,0:T(1,128)} %bitcast.20, f32[4,1,768]{2,1,0:T(1,128)} %bitcast.21, f32[4,1,768]{2,1,0:T(1,128)} %bitcast.22, f32[2,128]{1,0:T(2,128)} %bitcast.23, bf16[3,3072,128]{2,1,0:T(8,128)(2,1)} %bitcast.15, ...), custom_call_target="tpu_custom_call" | custom-call | tf_op jit(solution)/shard_map/pallas_call | solution.py:290
  353.1 1.1 copy.16
  354.2 0.8 reshape.21
  355.1 1.7 copy.21

commit v3 on v2

--- a/solution.py
+++ b/solution.py
@@ -16,7 +16,7 @@
     hid, shift, scale, gate, gain, w_hbm, o, st, bo_out, fc_out,
     xp, nga, ngb, xr, sg, kv, qb, og, att, atg, xo, bob, fcs, fcb,
     s_st, r_st, s_o, r_o, s_xp, r_xp, s_xr, r_xr, s_1a, r_1a, s_1b, r_1b,
-    s_2a, r_2a, s_2b, r_2b, s_at, r_at, s_fc, r_fc, s_bo, r_bo, w, s_w, go,
+    s_2a, r_2a, s_2b, r_2b, s_at, r_at, s_fc, r_fc, s_bo, r_bo, w, s_w, go, pa, pb,
 ):
     l = lax.axis_index("pipe")
     h = lax.axis_index("seq")
@@ -24,17 +24,16 @@
     count = lax.axis_size("seq")
     i = lax.div(h, SIDE)
     j = lax.rem(h, SIDE)
-    half = w.shape[1] // 2
+    half = w.shape[0] // 2
     rows, piece = xp.shape[2], xp.shape[3]
     group = SIDE * rows
     hs = gain.shape[1]
     factor = 1.0 / math.sqrt(hs)
     nxt = lax.rem(l + 1, sections)
     prv = lax.rem(l + sections - 1, sections)
-    even = lax.rem(l, 2) == 0
     partner = l + 1 - 2 * lax.rem(l, 2)
-    load_w = pltpu.make_async_copy(w_hbm, w, s_w)
-    load_w.start()
+    for m in range(3):
+        pltpu.make_async_copy(w_hbm.at[m], w.at[:, pl.ds(m * hs, hs)], s_w).start()
 
     def send(src, dst, ssem, rsem, pipe, seq):
         pltpu.make_async_remote_copy(
@@ -90,13 +89,11 @@
     def _():
         send_stale()
 
-    @pl.when((l > 0) & even)
+    @pl.when(l > 1)
     def _():
         send_out_proj(0, everyone)
-        await_bytes(og, r_o)
-        tell_partner()
-
-    @pl.when(lax.rem(l, 2) == 1)
+
+    @pl.when(l == 1)
     def _():
         pl.semaphore_wait(go, 1)
         send_out_proj(0, everyone // 2)
@@ -114,23 +111,26 @@
         nga[p, i, j, :, piece:] = normed[1]
         ngb[p, j, i, :, :piece] = normed[2]
         ngb[p, j, i, :, piece:] = normed[3]
-        @pl.when((p == 1) & even)
-        def _():
-            pl.semaphore_wait(go, 1)
-
-        for k in (2, 1, 3):
+        for k in (1, 3, 2):
             jj = lax.rem(j + k, SIDE)
             ii = lax.rem(i + k, SIDE)
-            send(nga.at[p, i, j], nga.at[p, i, j], s_1a.at[p], r_1a.at[p], l, SIDE * i + jj)
-            send(ngb.at[p, j, i], ngb.at[p, j, i], s_1b.at[p], r_1b.at[p], l, SIDE * ii + j)
-        await_bytes(nga.at[p, 0, pl.ds(0, SIDE - 1)], r_1a.at[p])
-        for k in (2, 1, 3):
+            send(nga.at[p, i, j], nga.at[p, i, j], s_1a.at[p], r_1a.at[p, j], l, SIDE * i + jj)
+            send(ngb.at[p, j, i], ngb.at[p, j, i], s_1b.at[p], r_1b.at[p, i], l, SIDE * ii + j)
+
+        def forward(isrc, jsrc):
+            for k in (1, 3, 2):
+                jj = lax.rem(j + k, SIDE)
+                ii = lax.rem(i + k, SIDE)
+                send(nga.at[p, i, jsrc], nga.at[p, i, jsrc], s_2a.at[p], r_2a.at[p, i], l, SIDE * ii + j)
+                send(ngb.at[p, j, isrc], ngb.at[p, j, isrc], s_2b.at[p], r_2b.at[p, j], l, SIDE * i + jj)
+
+        forward(i, j)
+        for k in (1, 3, 2):
+            jj = lax.rem(j + k, SIDE)
             ii = lax.rem(i + k, SIDE)
-            send(nga.at[p, i], nga.at[p, i], s_2a.at[p], r_2a.at[p], l, SIDE * ii + j)
-        await_bytes(ngb.at[p, 0, pl.ds(0, SIDE - 1)], r_1b.at[p])
-        for k in (2, 1, 3):
-            jj = lax.rem(j + k, SIDE)
-            send(ngb.at[p, j], ngb.at[p, j], s_2b.at[p], r_2b.at[p], l, SIDE * i + jj)
+            await_bytes(nga.at[p, i, jj], r_1a.at[p, jj])
+            await_bytes(ngb.at[p, j, ii], r_1b.at[p, ii])
+            forward(ii, jj)
         for k in range(1, SIDE):
             jj = lax.rem(j + k, SIDE)
             send(xp.at[p, jj], xr.at[p, j], s_xr.at[p], r_xr.at[p], l, SIDE * i + jj)
@@ -141,33 +141,47 @@
             send_stale()
             send_out_proj(0, everyone)
 
-        @pl.when((lax.rem(l, 2) == 1) & (p == 0))
+        @pl.when((l == 1) & (p == 0))
         def _():
             send_out_proj(everyone // 2, everyone)
 
         @pl.when(p == 0)
         def _():
-            load_w.wait()
+            await_bytes(w, s_w)
             await_bytes(sg, r_st)
             for c in range(2):
                 old = sg[:, c].astype(jnp.float32).reshape(count * rows, hs)
                 kv[0, c] = old.astype(jnp.bfloat16)
 
-        await_bytes(nga.at[p, pl.ds(0, SIDE - 1)], r_2a.at[p])
-        await_bytes(ngb.at[p, pl.ds(0, SIDE - 1)], r_2b.at[p])
-
-        @pl.when((p == 0) & (lax.rem(l, 2) == 1))
-        def _():
-            tell_partner()
+        def arrive(step, c):
+            k = step + lax.div(step, 2) * (5 - 2 * step)
+            ii = lax.rem(i + k, SIDE)
+            jj = lax.rem(j + k, SIDE)
+
+            @pl.when(step > 0)
+            def _():
+                await_bytes(nga.at[p, ii], r_2a.at[p, ii])
+
+            left = jnp.concatenate([nga[p, ii, m].astype(jnp.float32) for m in range(SIDE)], axis=0)
+            pa[ii] = jnp.dot(
+                left.astype(jnp.bfloat16), w[:half], preferred_element_type=jnp.float32
+            )
+
+            @pl.when(step > 0)
+            def _():
+                await_bytes(ngb.at[p, jj], r_2b.at[p, jj])
+
+            right = jnp.concatenate([ngb[p, jj, m].astype(jnp.float32) for m in range(SIDE)], axis=0)
+            right = jnp.dot(
+                right.astype(jnp.bfloat16), w[half:], preferred_element_type=jnp.float32
+            )
+            pb[jj] = right.reshape(SIDE, rows, 3 * hs)
+            return c
+
+        lax.fori_loop(0, SIDE, arrive, 0)
 
         def project(g, c):
-            left = jnp.concatenate([nga[p, g, m].astype(jnp.float32) for m in range(SIDE)], axis=0)
-            right = jnp.concatenate([ngb[p, m, g].astype(jnp.float32) for m in range(SIDE)], axis=0)
-            first = jnp.concatenate([w[m, :half] for m in range(3)], axis=1)
-            second = jnp.concatenate([w[m, half:] for m in range(3)], axis=1)
-            out = jnp.dot(
-                left.astype(jnp.bfloat16), first, preferred_element_type=jnp.float32
-            ) + jnp.dot(right.astype(jnp.bfloat16), second, preferred_element_type=jnp.float32)
+            out = pa[g] + pb[:, g].reshape(group, 3 * hs)
             for c in range(2):
                 part = out[:, c * hs : (c + 1) * hs]
                 square = jnp.mean(part * part, axis=-1, keepdims=True)
@@ -213,7 +227,7 @@
             send(fcs.at[p, t], fcb.at[p, h], s_fc.at[p], r_fc.at[p], l, t)
         local(fcs.at[p, h], fcb.at[p, h], r_fc.at[p])
 
-        @pl.when((p == 0) & ((l == 0) | (lax.rem(l, 2) == 1)))
+        @pl.when(p == 0)
         def _():
             await_bytes(og, r_o)
 
@@ -287,6 +301,7 @@
     hbm = pl.BlockSpec(memory_space=pl.ANY)
     one = pltpu.SemaphoreType.DMA
     pair = pltpu.SemaphoreType.DMA((2,))
+    quad = pltpu.SemaphoreType.DMA((2, SIDE))
     bo, fc = pl.pallas_call(
         block_kernel,
         out_shape=(
@@ -311,10 +326,12 @@
             pltpu.VMEM((patches, count, 2, rows, hs), bf),
             pltpu.VMEM((patches, count, 2, rows, hs), bf),
             one, one, one, one,
-        ] + [pair] * 18 + [
-            pltpu.VMEM((3, width, hs), bf),
+        ] + [pair] * 4 + [pair, quad] * 4 + [pair] * 6 + [
+            pltpu.VMEM((width, 3 * hs), bf),
             one,
             pltpu.SemaphoreType.REGULAR,
+            pltpu.VMEM((SIDE, SIDE * rows, 3 * hs), f32),
+            pltpu.VMEM((SIDE, SIDE, rows, 3 * hs), f32),
         ],
         compiler_params=pltpu.CompilerParams(
             collective_id=0, has_side_effects=True, vmem_limit_bytes=56 * 1024 * 1024

time: 357 us -> 298 us (0.83)
  Pallas kernels: 351 us -> 292 us
    pallas_call x1, Pallas kernels: 351 us -> 292 us  [body(): pl.pallas_call(block_kernel, out_shape=(jax.ShapeDtypeStruct((patches, ro...]
where the time goes in v3:
time: 298 us
  Pallas kernels  292 us (98%)
  local copies, waits for them, and re-layouts  5.58 us (2%)
    pallas_call x1, Pallas kernels, body(): pl.pallas_call(block_kernel, out_shape=(jax.ShapeDtypeStruct((patches, ro...  292 us

profile of v3, /device:TPU:25, one launch (start us, length us, event | category | flops | bytes accessed | tf_op | source)
XLA Modules:
  0.0 297.8 jit_solution(3262392645997570374)
XLA Ops:
  0.6 1.1 slice.3
  1.7 0.1 reshape.20
  1.8 0.8 copy.19
  2.6 291.5 %shard_map.95 = (bf16[2,24,3072]{2,1,0:T(8,128)(2,1)}, bf16[2,16,2,24,128]{4,3,2,1,0:T(8,128)(2,1)}) custom-call(bf16[2,24,3072]{2,1,0:T(8,128)(2,1)} %hid.1, f32[4,1,768]{2,1,0:T(1,128)} %bitcast.20, f32[4,1,768]{2,1,0:T(1,128)} %bitcast.21, f32[4,1,768]{2,1,0:T(1,128)} %bitcast.22, f32[2,128]{1,0:T(2,128)} %bitcast.23, bf16[3,3072,128]{2,1,0:T(8,128)(2,1)} %bitcast.15, ...), custom_call_target="tpu_custom_call" | custom-call | tf_op jit(solution)/shard_map/pallas_call | solution.py:305
  294.1 1.1 copy.16
  295.2 0.8 reshape.21
  296.1 1.7 copy.21

commit v4 on v3

--- a/solution.py
+++ b/solution.py
@@ -17,6 +17,7 @@
     xp, nga, ngb, xr, sg, kv, qb, og, att, atg, xo, bob, fcs, fcb,
     s_st, r_st, s_o, r_o, s_xp, r_xp, s_xr, r_xr, s_1a, r_1a, s_1b, r_1b,
     s_2a, r_2a, s_2b, r_2b, s_at, r_at, s_fc, r_fc, s_bo, r_bo, w, s_w, go, pa, pb,
+    up, prs, rs, s_rs, r_rs,
 ):
     l = lax.axis_index("pipe")
     h = lax.axis_index("seq")
@@ -31,7 +32,8 @@
     factor = 1.0 / math.sqrt(hs)
     nxt = lax.rem(l + 1, sections)
     prv = lax.rem(l + sections - 1, sections)
-    partner = l + 1 - 2 * lax.rem(l, 2)
+    odd = lax.rem(l, 2) == 1
+    early = l < 2
     for m in range(3):
         pltpu.make_async_copy(w_hbm.at[m], w.at[:, pl.ds(m * hs, hs)], s_w).start()
 
@@ -65,17 +67,13 @@
 
     pl.semaphore_wait(barrier, SIDE * SIDE - 1 + 2 * SIDE)
 
-    def send_out_proj(first, last):
-        for k in range(max(first, 1), last):
+    def send_out_proj():
+        for k in range(1, SIDE * SIDE):
             t = other(k)
             col = pl.multiple_of(lax.rem(t, SIDE) * piece, 128)
             send(o.at[:, pl.ds(col, piece)], og.at[h], s_o, r_o, l, t)
-        if first == 0:
-            col = pl.multiple_of(j * piece, 128)
-            local(o.at[:, pl.ds(col, piece)], og.at[h], r_o)
-
-    def tell_partner():
-        pl.semaphore_signal(go, inc=1, device_id=(partner, h), device_id_type=MESH)
+        col = pl.multiple_of(j * piece, 128)
+        local(o.at[:, pl.ds(col, piece)], og.at[h], r_o)
 
     def send_stale():
         for k in range(1, SIDE * SIDE):
@@ -83,22 +81,15 @@
             send(st.at[t], sg.at[h], s_st, r_st, l, t)
         local(st.at[h], sg.at[h], r_st)
 
-    everyone = SIDE * SIDE
-
     @pl.when(l > 0)
     def _():
         send_stale()
 
-    @pl.when(l > 1)
-    def _():
-        send_out_proj(0, everyone)
-
-    @pl.when(l == 1)
-    def _():
-        pl.semaphore_wait(go, 1)
-        send_out_proj(0, everyone // 2)
-
-    def patch(p, carry):
+    @pl.when(~early)
+    def _():
+        send_out_proj()
+
+    def start(p):
         await_bytes(xp.at[p], r_xp.at[p])
         x = xp[p].astype(jnp.float32)
         width = SIDE * piece
@@ -117,42 +108,49 @@
             send(nga.at[p, i, j], nga.at[p, i, j], s_1a.at[p], r_1a.at[p, j], l, SIDE * i + jj)
             send(ngb.at[p, j, i], ngb.at[p, j, i], s_1b.at[p], r_1b.at[p, i], l, SIDE * ii + j)
 
-        def forward(isrc, jsrc):
-            for k in (1, 3, 2):
-                jj = lax.rem(j + k, SIDE)
-                ii = lax.rem(i + k, SIDE)
-                send(nga.at[p, i, jsrc], nga.at[p, i, jsrc], s_2a.at[p], r_2a.at[p, i], l, SIDE * ii + j)
-                send(ngb.at[p, j, isrc], ngb.at[p, j, isrc], s_2b.at[p], r_2b.at[p, j], l, SIDE * i + jj)
-
-        forward(i, j)
+        forward(p, i, j)
+
+    def forward(p, isrc, jsrc):
+        for k in (1, 3, 2):
+            jj = lax.rem(j + k, SIDE)
+            ii = lax.rem(i + k, SIDE)
+            send(nga.at[p, i, jsrc], nga.at[p, i, jsrc], s_2a.at[p], r_2a.at[p, i], l, SIDE * ii + j)
+            send(ngb.at[p, j, isrc], ngb.at[p, j, isrc], s_2b.at[p], r_2b.at[p, j], l, SIDE * i + jj)
+
+    def relay(p):
         for k in (1, 3, 2):
             jj = lax.rem(j + k, SIDE)
             ii = lax.rem(i + k, SIDE)
             await_bytes(nga.at[p, i, jj], r_1a.at[p, jj])
             await_bytes(ngb.at[p, j, ii], r_1b.at[p, ii])
-            forward(ii, jj)
+            forward(p, ii, jj)
         for k in range(1, SIDE):
             jj = lax.rem(j + k, SIDE)
             send(xp.at[p, jj], xr.at[p, j], s_xr.at[p], r_xr.at[p], l, SIDE * i + jj)
         local(xp.at[p, j], xr.at[p, j], r_xr.at[p])
 
-        @pl.when((l == 0) & (p == 0))
+
+    def settle():
+        @pl.when(l == 0)
         def _():
             send_stale()
-            send_out_proj(0, everyone)
-
-        @pl.when((l == 1) & (p == 0))
+
+        @pl.when(early)
         def _():
-            send_out_proj(everyone // 2, everyone)
-
-        @pl.when(p == 0)
-        def _():
-            await_bytes(w, s_w)
-            await_bytes(sg, r_st)
-            for c in range(2):
-                old = sg[:, c].astype(jnp.float32).reshape(count * rows, hs)
-                kv[0, c] = old.astype(jnp.bfloat16)
-
+            for k in range(1, SIDE):
+                jj = lax.rem(j + k, SIDE)
+                col = pl.multiple_of(jj * piece, 128)
+                send(o.at[:, pl.ds(col, piece)], og.at[j], s_o, r_o, l, SIDE * i + jj)
+            col = pl.multiple_of(j * piece, 128)
+            local(o.at[:, pl.ds(col, piece)], og.at[j], r_o)
+
+        await_bytes(w, s_w)
+        await_bytes(sg, r_st)
+        for c in range(2):
+            old = sg[:, c].astype(jnp.float32).reshape(count * rows, hs)
+            kv[0, c] = old.astype(jnp.bfloat16)
+
+    def project(p):
         def arrive(step, c):
             k = step + lax.div(step, 2) * (5 - 2 * step)
             ii = lax.rem(i + k, SIDE)
@@ -180,7 +178,7 @@
 
         lax.fori_loop(0, SIDE, arrive, 0)
 
-        def project(g, c):
+        def heads(g, c):
             out = pa[g] + pb[:, g].reshape(group, 3 * hs)
             for c in range(2):
                 part = out[:, c * hs : (c + 1) * hs]
@@ -197,9 +195,10 @@
             fcs[p, pl.ds(g * SIDE, SIDE), 1] = values.reshape(SIDE, rows, hs).astype(jnp.bfloat16)
             return c
 
-        lax.fori_loop(0, SIDE, project, 0)
-
-        def attend(g):
+        lax.fori_loop(0, SIDE, heads, 0)
+
+    def attend(p):
+        def one(g):
             q = qb[g]
             dims = (((1,), (1,)), ((), ()))
             near = lax.dot_general(q, kv[p + 1, 0], dims, preferred_element_type=jnp.float32)
@@ -216,47 +215,103 @@
 
         for gg in (2, 1, 3, 0):
             g = lax.rem(i + gg, SIDE)
-            attend(g)
-            for k in range(1 if gg == 0 else 0, SIDE):
-                jj = lax.rem(j + k, SIDE)
-                send(att.at[p, g], atg.at[p, h], s_at.at[p], r_at.at[p], l, SIDE * g + jj)
-        local(att.at[p, i], atg.at[p, h], r_at.at[p])
-
+            one(g)
+
+            @pl.when(early)
+            def _():
+                for k in range(1, SIDE):
+                    jj = lax.rem(j + k, SIDE)
+                    send(att.at[p, g], atg.at[p, SIDE * j + g], s_at.at[p], r_at.at[p], l, SIDE * i + jj)
+                local(att.at[p, g], atg.at[p, SIDE * j + g], r_at.at[p])
+
+            @pl.when(~early)
+            def _():
+                for k in range(1 if gg == 0 else 0, SIDE):
+                    jj = lax.rem(j + k, SIDE)
+                    send(att.at[p, g], atg.at[p, h], s_at.at[p], r_at.at[p], l, SIDE * g + jj)
+                if gg == 0:
+                    local(att.at[p, g], atg.at[p, h], r_at.at[p])
+
+    def by_heads(p):
+        if p == 0:
+            await_bytes(og.at[pl.ds(0, SIDE)], r_o)
+        weight = og[0:SIDE].reshape(SIDE * hs, piece)
+        await_bytes(atg.at[p], r_at.at[p])
+        for gg in (2, 1, 3, 0):
+            g = lax.rem(i + gg, SIDE)
+            mixed = jnp.concatenate([atg[p, SIDE * m + g] for m in range(SIDE)], axis=1)
+            part = jnp.dot(mixed, weight, preferred_element_type=jnp.float32)
+            if gg == 0:
+                up[...] = part
+            else:
+                prs[p, g] = part.astype(jnp.bfloat16)
+                send(prs.at[p, g], rs.at[p, i], s_rs.at[p], r_rs.at[p], l, SIDE * g + j)
+        await_bytes(rs.at[p, pl.ds(0, SIDE - 1)], r_rs.at[p])
+        total = up[...]
+        for gg in range(1, SIDE):
+            total = total + rs[p, lax.rem(i + gg, SIDE)].astype(jnp.float32)
+        up[...] = total
+
+    def by_tokens(p):
+        if p == 0:
+            await_bytes(og, r_o)
+        await_bytes(atg.at[p], r_at.at[p])
+        mixed = jnp.concatenate([atg[p, m] for m in range(SIDE * SIDE)], axis=1)
+        up[...] = jnp.dot(
+            mixed, og[...].reshape(SIDE * SIDE * hs, piece), preferred_element_type=jnp.float32
+        )
+
+    def finish(p):
+        await_bytes(xr.at[p], r_xr.at[p])
+
+        @pl.when(early)
+        def _():
+            by_heads(p)
+
+        @pl.when(~early)
+        def _():
+            by_tokens(p)
+
+        base = xr[p].astype(jnp.float32).reshape(group, piece)
+        result = base + gate[j] * up[...]
+        xo[p] = result.reshape(SIDE, rows, piece).astype(jnp.bfloat16)
+
+        @pl.when(l < sections - 1)
+        def _():
+            for k in range(SIDE):
+                send(xo.at[p, k], xp.at[p, j], s_xp.at[p], r_xp.at[p], nxt, SIDE * i + k)
+
+        for k in range(1, SIDE):
+            kk = lax.rem(j + k, SIDE)
+            send(xo.at[p, kk], bob.at[p, j], s_bo.at[p], r_bo.at[p], l, SIDE * i + kk)
+        local(xo.at[p, j], bob.at[p, j], r_bo.at[p])
         for k in range(1, SIDE * SIDE):
             t = other(k)
             send(fcs.at[p, t], fcb.at[p, h], s_fc.at[p], r_fc.at[p], l, t)
         local(fcs.at[p, h], fcb.at[p, h], r_fc.at[p])
 
-        @pl.when(p == 0)
-        def _():
-            await_bytes(og, r_o)
-
-        @pl.when((p == 0) & (l == 0))
-        def _():
-            tell_partner()
-
-        await_bytes(xr.at[p], r_xr.at[p])
-        base = xr[p].astype(jnp.float32).reshape(group, piece)
-        await_bytes(atg.at[p], r_at.at[p])
-        mixed = jnp.concatenate([atg[p, m] for m in range(SIDE * SIDE)], axis=1)
-        update = jnp.dot(
-            mixed, og[...].reshape(SIDE * SIDE * hs, piece), preferred_element_type=jnp.float32
-        )
-        result = base + gate[j] * update
-        xo[p] = result.reshape(SIDE, rows, piece).astype(jnp.bfloat16)
-
-        @pl.when(l < sections - 1)
-        def _():
-            for k in range(SIDE):
-                send(xo.at[p, k], xp.at[p, j], s_xp.at[p], r_xp.at[p], nxt, SIDE * i + k)
-
-        for k in range(1, SIDE):
-            kk = lax.rem(j + k, SIDE)
-            send(xo.at[p, kk], bob.at[p, j], s_bo.at[p], r_bo.at[p], l, SIDE * i + kk)
-        local(xo.at[p, j], bob.at[p, j], r_bo.at[p])
-        return carry
-
-    lax.fori_loop(0, 2, patch, 0)
+    start(0)
+    relay(0)
+    settle()
+
+    @pl.when(odd)
+    def _():
+        pl.semaphore_signal(go, inc=1, device_id=(prv, h), device_id_type=MESH)
+
+    project(0)
+
+    attend(0)
+    finish(0)
+
+    @pl.when(~odd)
+    def _():
+        pl.semaphore_wait(go, 1)
+
+    start(1)
+    relay(1)
+    project(1)
+    attend(1)
+    finish(1)
 
     for p in range(2):
         await_bytes(fcb.at[p], r_fc.at[p])
@@ -268,16 +323,27 @@
     most = pl.ds(0, SIDE * SIDE - 1)
     three = pl.ds(0, SIDE - 1)
     await_bytes(sg.at[most], s_st)
-    await_bytes(og.at[most], s_o)
     for p in range(2):
         await_bytes(nga.at[p, 0, three], s_1a.at[p])
         await_bytes(ngb.at[p, 0, three], s_1b.at[p])
         await_bytes(nga.at[p, three], s_2a.at[p])
         await_bytes(ngb.at[p, three], s_2b.at[p])
         await_bytes(xr.at[p, three], s_xr.at[p])
-        await_bytes(atg.at[p, most], s_at.at[p])
         await_bytes(fcb.at[p, most], s_fc.at[p])
         await_bytes(bob.at[p, three], s_bo.at[p])
+
+    @pl.when(early)
+    def _():
+        await_bytes(og.at[three], s_o)
+        for p in range(2):
+            await_bytes(atg.at[p, pl.ds(0, SIDE * (SIDE - 1))], s_at.at[p])
+            await_bytes(rs.at[p, three], s_rs.at[p])
+
+    @pl.when(~early)
+    def _():
+        await_bytes(og.at[most], s_o)
+        for p in range(2):
+            await_bytes(atg.at[p, most], s_at.at[p])
 
     @pl.when(l < sections - 1)
     def _():
@@ -332,6 +398,10 @@
             pltpu.SemaphoreType.REGULAR,
             pltpu.VMEM((SIDE, SIDE * rows, 3 * hs), f32),
             pltpu.VMEM((SIDE, SIDE, rows, 3 * hs), f32),
+            pltpu.VMEM((SIDE * rows, piece), f32),
+            pltpu.VMEM((patches, SIDE, SIDE * rows, piece), bf),
+            pltpu.VMEM((patches, SIDE, SIDE * rows, piece), bf),
+            pair, pair,
         ],
         compiler_params=pltpu.CompilerParams(
             collective_id=0, has_side_effects=True, vmem_limit_bytes=56 * 1024 * 1024

time: 298 us -> 273 us (0.916)
  Pallas kernels: 292 us -> 267 us
    pallas_call x1, Pallas kernels: 292 us -> 267 us  [body(): pl.pallas_call(block_kernel, out_shape=(jax.ShapeDtypeStruct((patches, ro...]
where the time goes in v4:
time: 273 us
  Pallas kernels  267 us (98%)
  local copies, waits for them, and re-layouts  5.58 us (2%)
    pallas_call x1, Pallas kernels, body(): pl.pallas_call(block_kernel, out_shape=(jax.ShapeDtypeStruct((patches, ro...  267 us

profile of v4, /device:TPU:25, one launch (start us, length us, event | category | flops | bytes accessed | tf_op | source)
XLA Modules:
  0.0 273.0 jit_solution(10619560565782138090)
XLA Ops:
  0.6 1.1 slice.3
  1.7 0.1 reshape.20
  1.8 0.8 copy.19
  2.6 266.8 %shard_map.95 = (bf16[2,24,3072]{2,1,0:T(8,128)(2,1)}, bf16[2,16,2,24,128]{4,3,2,1,0:T(8,128)(2,1)}) custom-call(bf16[2,24,3072]{2,1,0:T(8,128)(2,1)} %hid.1, f32[4,1,768]{2,1,0:T(1,128)} %bitcast.20, f32[4,1,768]{2,1,0:T(1,128)} %bitcast.21, f32[4,1,768]{2,1,0:T(1,128)} %bitcast.22, f32[2,128]{1,0:T(2,128)} %bitcast.23, bf16[3,3072,128]{2,1,0:T(8,128)(2,1)} %bitcast.15, ...), custom_call_target="tpu_custom_call" | custom-call | tf_op jit(solution)/shard_map/pallas_call | solution.py:371
  269.4 1.1 copy.16
  270.5 0.8 reshape.21
  271.3 1.7 copy.21

commit v5 on v4

--- a/solution.py
+++ b/solution.py
@@ -75,19 +75,30 @@
         col = pl.multiple_of(j * piece, 128)
         local(o.at[:, pl.ds(col, piece)], og.at[h], r_o)
 
+    def send_rows():
+        for k in range(1, SIDE):
+            jj = lax.rem(j + k, SIDE)
+            col = pl.multiple_of(jj * piece, 128)
+            send(o.at[:, pl.ds(col, piece)], og.at[j], s_o, r_o, l, SIDE * i + jj)
+        col = pl.multiple_of(j * piece, 128)
+        local(o.at[:, pl.ds(col, piece)], og.at[j], r_o)
+
     def send_stale():
         for k in range(1, SIDE * SIDE):
             t = other(k)
             send(st.at[t], sg.at[h], s_st, r_st, l, t)
         local(st.at[h], sg.at[h], r_st)
 
-    @pl.when(l > 0)
-    def _():
-        send_stale()
+    send_stale()
 
     @pl.when(~early)
     def _():
         send_out_proj()
+
+    @pl.when(l == 1)
+    def _():
+        pl.semaphore_wait(go, 1)
+        send_rows()
 
     def start(p):
         await_bytes(xp.at[p], r_xp.at[p])
@@ -133,16 +144,7 @@
     def settle():
         @pl.when(l == 0)
         def _():
-            send_stale()
-
-        @pl.when(early)
-        def _():
-            for k in range(1, SIDE):
-                jj = lax.rem(j + k, SIDE)
-                col = pl.multiple_of(jj * piece, 128)
-                send(o.at[:, pl.ds(col, piece)], og.at[j], s_o, r_o, l, SIDE * i + jj)
-            col = pl.multiple_of(j * piece, 128)
-            local(o.at[:, pl.ds(col, piece)], og.at[j], r_o)
+            send_rows()
 
         await_bytes(w, s_w)
         await_bytes(sg, r_st)
@@ -285,6 +287,8 @@
             kk = lax.rem(j + k, SIDE)
             send(xo.at[p, kk], bob.at[p, j], s_bo.at[p], r_bo.at[p], l, SIDE * i + kk)
         local(xo.at[p, j], bob.at[p, j], r_bo.at[p])
+
+    def send_cache(p):
         for k in range(1, SIDE * SIDE):
             t = other(k)
             send(fcs.at[p, t], fcb.at[p, h], s_fc.at[p], r_fc.at[p], l, t)
@@ -303,6 +307,11 @@
     attend(0)
     finish(0)
 
+    @pl.when(l == 0)
+    def _():
+        pl.semaphore_signal(go, inc=1, device_id=(nxt, h), device_id_type=MESH)
+
+
     @pl.when(~odd)
     def _():
         pl.semaphore_wait(go, 1)
@@ -311,7 +320,9 @@
     relay(1)
     project(1)
     attend(1)
+    send_cache(0)
     finish(1)
+    send_cache(1)
 
     for p in range(2):
         await_bytes(fcb.at[p], r_fc.at[p])
@@ -319,7 +330,7 @@
     fc_out[...] = fcb[...]
     for p in range(2):
         for q in range(SIDE):
-            bo_out[p, :, q * piece : (q + 1) * piece] = bob[p, q]
+            bo_out[p, :, q * piece : (q + 1) * piece] = bob[p, q].astype(jnp.float32)
     most = pl.ds(0, SIDE * SIDE - 1)
     three = pl.ds(0, SIDE - 1)
     await_bytes(sg.at[most], s_st)
@@ -371,7 +382,7 @@
     bo, fc = pl.pallas_call(
         block_kernel,
         out_shape=(
-            jax.ShapeDtypeStruct((patches, rows, width), bf),
+            jax.ShapeDtypeStruct((patches, rows, width), f32),
             jax.ShapeDtypeStruct((patches, count, 2, rows, hs), bf),
         ),
         in_specs=[vmem] * 5 + [hbm, hbm, vmem],
@@ -407,7 +418,7 @@
             collective_id=0, has_side_effects=True, vmem_limit_bytes=56 * 1024 * 1024
         ),
     )(hidden, shift, scale, gate, norm_gain[0], w, output_proj[0], st)
-    outputs = bo[None]
+    outputs = bo.astype(bf)[None]
     cache = fc.transpose(0, 3, 2, 1, 4).reshape(1, patches, rows, 2, count * hs)
     return outputs, cache
 

time: 273 us -> 268 us (0.982)
  Pallas kernels: 267 us -> 262 us
    pallas_call x1, Pallas kernels: 267 us -> 262 us  [body(): pl.pallas_call(block_kernel, out_shape=(jax.ShapeDtypeStruct((patches, ro...]
where the time goes in v5:
time: 268 us
  Pallas kernels  262 us (98%)
  local copies, waits for them, and re-layouts  3.89 us (1%)
    pallas_call x1, Pallas kernels, body(): pl.pallas_call(block_kernel, out_shape=(jax.ShapeDtypeStruct((patches, ro...  262 us

profile of v5, /device:TPU:25, one launch (start us, length us, event | category | flops | bytes accessed | tf_op | source)
XLA Modules:
  0.0 268.2 jit_solution(6572088965340683510)
XLA Ops:
  0.6 1.1 slice.3
  1.7 0.1 reshape.20
  1.8 0.8 copy.19
  2.6 261.9 %shard_map.95 = (f32[2,24,3072]{2,1,0:T(8,128)}, bf16[2,16,2,24,128]{4,3,2,1,0:T(8,128)(2,1)}) custom-call(bf16[2,24,3072]{2,1,0:T(8,128)(2,1)} %hid.1, f32[4,1,768]{2,1,0:T(1,128)} %bitcast.20, f32[4,1,768]{2,1,0:T(1,128)} %bitcast.21, f32[4,1,768]{2,1,0:T(1,128)} %bitcast.22, f32[2,128]{1,0:T(2,128)} %bitcast.23, bf16[3,3072,128]{2,1,0:T(8,128)(2,1)} %bitcast.16, ...), custom_call_target="tpu_custom_call" | custom-call | tf_op jit(solution)/shard_map/pallas_call | solution.py:382
  264.5 1.8 convert_bitcast_fusion
  266.3 1.1 copy.16
  267.4 0.8 reshape.21

commit v6 on v5

--- a/solution.py
+++ b/solution.py
@@ -113,6 +113,8 @@
         nga[p, i, j, :, piece:] = normed[1]
         ngb[p, j, i, :, :piece] = normed[2]
         ngb[p, j, i, :, piece:] = normed[3]
+
+    def own_blocks(p):
         for k in (1, 3, 2):
             jj = lax.rem(j + k, SIDE)
             ii = lax.rem(i + k, SIDE)
@@ -178,7 +180,7 @@
             pb[jj] = right.reshape(SIDE, rows, 3 * hs)
             return c
 
-        lax.fori_loop(0, SIDE, arrive, 0)
+        lax.fori_loop(0, SIDE, arrive, 0, unroll=True)
 
         def heads(g, c):
             out = pa[g] + pb[:, g].reshape(group, 3 * hs)
@@ -197,7 +199,7 @@
             fcs[p, pl.ds(g * SIDE, SIDE), 1] = values.reshape(SIDE, rows, hs).astype(jnp.bfloat16)
             return c
 
-        lax.fori_loop(0, SIDE, heads, 0)
+        lax.fori_loop(0, SIDE, heads, 0, unroll=True)
 
     def attend(p):
         def one(g):
@@ -295,6 +297,7 @@
         local(fcs.at[p, h], fcb.at[p, h], r_fc.at[p])
 
     start(0)
+    own_blocks(0)
     relay(0)
     settle()
 
@@ -311,12 +314,13 @@
     def _():
         pl.semaphore_signal(go, inc=1, device_id=(nxt, h), device_id_type=MESH)
 
+    start(1)
 
     @pl.when(~odd)
     def _():
         pl.semaphore_wait(go, 1)
 
-    start(1)
+    own_blocks(1)
     relay(1)
     project(1)
     attend(1)

time: 268 us -> 264 us (0.985)
  Pallas kernels: 262 us -> 257 us
    pallas_call x1, Pallas kernels: 262 us -> 257 us  [body(): pl.pallas_call(block_kernel, out_shape=(jax.ShapeDtypeStruct((patches, ro...]
where the time goes in v6:
time: 264 us; the launch traced here: 263 us
  Pallas kernels  257 us (97%)
  local copies, waits for them, and re-layouts  3.89 us (1%)
    pallas_call x1, Pallas kernels, body(): pl.pallas_call(block_kernel, out_shape=(jax.ShapeDtypeStruct((patches, ro...  257 us

profile of v6, /device:TPU:25, one launch (start us, length us, event | category | flops | bytes accessed | tf_op | source)
XLA Modules:
  0.0 263.3 jit_solution(12719445648915044828)
XLA Ops:
  0.6 1.1 slice.3
  1.7 0.1 reshape.20
  1.8 0.8 copy.19
  2.6 257.0 %shard_map.95 = (f32[2,24,3072]{2,1,0:T(8,128)}, bf16[2,16,2,24,128]{4,3,2,1,0:T(8,128)(2,1)}) custom-call(bf16[2,24,3072]{2,1,0:T(8,128)(2,1)} %hid.1, f32[4,1,768]{2,1,0:T(1,128)} %bitcast.20, f32[4,1,768]{2,1,0:T(1,128)} %bitcast.21, f32[4,1,768]{2,1,0:T(1,128)} %bitcast.22, f32[2,128]{1,0:T(2,128)} %bitcast.23, bf16[3,3072,128]{2,1,0:T(8,128)(2,1)} %bitcast.16, ...), custom_call_target="tpu_custom_call" | custom-call | tf_op jit(solution)/shard_map/pallas_call | solution.py:386
  259.6 1.8 convert_bitcast_fusion
  261.4 1.1 copy.16
  262.5 0.8 reshape.21

commit v7 on v6

--- a/solution.py
+++ b/solution.py
@@ -152,7 +152,7 @@
         await_bytes(sg, r_st)
         for c in range(2):
             old = sg[:, c].astype(jnp.float32).reshape(count * rows, hs)
-            kv[0, c] = old.astype(jnp.bfloat16)
+            kv[c, 0] = old.astype(jnp.bfloat16)
 
     def project(p):
         def arrive(step, c):
@@ -193,8 +193,8 @@
                 else:
                     keys = part
             values = out[:, 2 * hs :]
-            kv[p + 1, 0, pl.ds(pl.multiple_of(g * group, group), group)] = keys.astype(jnp.bfloat16)
-            kv[p + 1, 1, pl.ds(pl.multiple_of(g * group, group), group)] = values.astype(jnp.bfloat16)
+            kv[0, p + 1, pl.ds(pl.multiple_of(g * group, group), group)] = keys.astype(jnp.bfloat16)
+            kv[1, p + 1, pl.ds(pl.multiple_of(g * group, group), group)] = values.astype(jnp.bfloat16)
             fcs[p, pl.ds(g * SIDE, SIDE), 0] = keys.reshape(SIDE, rows, hs).astype(jnp.bfloat16)
             fcs[p, pl.ds(g * SIDE, SIDE), 1] = values.reshape(SIDE, rows, hs).astype(jnp.bfloat16)
             return c
@@ -205,16 +205,13 @@
         def one(g):
             q = qb[g]
             dims = (((1,), (1,)), ((), ()))
-            near = lax.dot_general(q, kv[p + 1, 0], dims, preferred_element_type=jnp.float32)
-            far = lax.dot_general(q, kv[p, 0], dims, preferred_element_type=jnp.float32)
-            near = jnp.exp(near * factor)
-            far = jnp.exp(far * factor)
-            den = jnp.sum(near, axis=-1, keepdims=True) + jnp.sum(far, axis=-1, keepdims=True)
-            inv = 1.0 / den
-            near = (near * inv).astype(jnp.bfloat16)
-            far = (far * inv).astype(jnp.bfloat16)
-            mixed = jnp.dot(near, kv[p + 1, 1], preferred_element_type=jnp.float32)
-            mixed = mixed + jnp.dot(far, kv[p, 1], preferred_element_type=jnp.float32)
+            keys = kv[0, p : p + 2].reshape(2 * count * rows, hs)
+            values = kv[1, p : p + 2].reshape(2 * count * rows, hs)
+            weights = lax.dot_general(q, keys, dims, preferred_element_type=jnp.float32)
+            weights = jnp.exp(weights * factor)
+            inv = 1.0 / jnp.sum(weights, axis=-1, keepdims=True)
+            probs = (weights * inv).astype(jnp.bfloat16)
+            mixed = jnp.dot(probs, values, preferred_element_type=jnp.float32)
             att[p, g] = mixed.astype(jnp.bfloat16)
 
         for gg in (2, 1, 3, 0):
@@ -235,6 +232,11 @@
                     send(att.at[p, g], atg.at[p, h], s_at.at[p], r_at.at[p], l, SIDE * g + jj)
                 if gg == 0:
                     local(att.at[p, g], atg.at[p, h], r_at.at[p])
+
+    def add_up(p, update):
+        base = xr[p].astype(jnp.float32).reshape(group, piece)
+        result = base + gate[j] * update
+        xo[p] = result.reshape(SIDE, rows, piece).astype(jnp.bfloat16)
 
     def by_heads(p):
         if p == 0:
@@ -254,16 +256,16 @@
         total = up[...]
         for gg in range(1, SIDE):
             total = total + rs[p, lax.rem(i + gg, SIDE)].astype(jnp.float32)
-        up[...] = total
+        add_up(p, total)
 
     def by_tokens(p):
         if p == 0:
             await_bytes(og, r_o)
         await_bytes(atg.at[p], r_at.at[p])
         mixed = jnp.concatenate([atg[p, m] for m in range(SIDE * SIDE)], axis=1)
-        up[...] = jnp.dot(
-            mixed, og[...].reshape(SIDE * SIDE * hs, piece), preferred_element_type=jnp.float32
-        )
+        weight = og[...].reshape(SIDE * SIDE * hs, piece)
+        update = jnp.dot(mixed, weight, preferred_element_type=jnp.float32)
+        add_up(p, update)
 
     def finish(p):
         await_bytes(xr.at[p], r_xr.at[p])
@@ -275,10 +277,6 @@
         @pl.when(~early)
         def _():
             by_tokens(p)
-
-        base = xr[p].astype(jnp.float32).reshape(group, piece)
-        result = base + gate[j] * up[...]
-        xo[p] = result.reshape(SIDE, rows, piece).astype(jnp.bfloat16)
 
         @pl.when(l < sections - 1)
         def _():
@@ -325,8 +323,8 @@
     project(1)
     attend(1)
     send_cache(0)
+    send_cache(1)
     finish(1)
-    send_cache(1)
 
     for p in range(2):
         await_bytes(fcb.at[p], r_fc.at[p])
@@ -397,7 +395,7 @@
             pltpu.VMEM((patches, SIDE, SIDE, rows, half), bf),
             pltpu.VMEM((patches, SIDE, rows, piece), bf),
             pltpu.VMEM((count, 2, rows, hs), bf),
-            pltpu.VMEM((patches + 1, 2, count * rows, hs), bf),
+            pltpu.VMEM((2, patches + 1, count * rows, hs), bf),
             pltpu.VMEM((SIDE, SIDE * rows, hs), bf),
             pltpu.VMEM((count, hs, piece), bf),
             pltpu.VMEM((patches, SIDE, SIDE * rows, hs), bf),

time: 264 us -> 262 us (level)
  no operation moved by 1% of the time
where the time goes in v7:
time: 262 us
  Pallas kernels  256 us (98%)
  local copies, waits for them, and re-layouts  3.89 us (1%)
    pallas_call x1, Pallas kernels, body(): pl.pallas_call(block_kernel, out_shape=(jax.ShapeDtypeStruct((patches, ro...  256 us

profile of v7, /device:TPU:25, one launch (start us, length us, event | category | flops | bytes accessed | tf_op | source)
XLA Modules:
  0.0 262.1 jit_solution(16429230394999980396)
XLA Ops:
  0.6 1.1 slice.3
  1.7 0.1 reshape.20
  1.8 0.8 copy.19
  2.6 255.8 %shard_map.95 = (f32[2,24,3072]{2,1,0:T(8,128)}, bf16[2,16,2,24,128]{4,3,2,1,0:T(8,128)(2,1)}) custom-call(bf16[2,24,3072]{2,1,0:T(8,128)(2,1)} %hid.1, f32[4,1,768]{2,1,0:T(1,128)} %bitcast.20, f32[4,1,768]{2,1,0:T(1,128)} %bitcast.21, f32[4,1,768]{2,1,0:T(1,128)} %bitcast.22, f32[2,128]{1,0:T(2,128)} %bitcast.23, bf16[3,3072,128]{2,1,0:T(8,128)(2,1)} %bitcast.16, ...), custom_call_target="tpu_custom_call" | custom-call | tf_op jit(solution)/shard_map/pallas_call | solution.py:384
  258.4 1.8 convert_bitcast_fusion
  260.2 1.1 copy.16
  261.3 0.8 reshape.21

commit v8 on v7

--- a/solution.py
+++ b/solution.py
@@ -387,7 +387,7 @@
             jax.ShapeDtypeStruct((patches, rows, width), f32),
             jax.ShapeDtypeStruct((patches, count, 2, rows, hs), bf),
         ),
-        in_specs=[vmem] * 5 + [hbm, hbm, vmem],
+        in_specs=[hbm] + [vmem] * 4 + [hbm] * 3,
         out_specs=(vmem, vmem),
         scratch_shapes=[
             pltpu.VMEM((patches, SIDE, rows, piece), bf),

time: 262 us -> 263 us (level)
  no operation moved by 1% of the time
where the time goes in v8:
time: 263 us; the launch traced here: 262 us
  Pallas kernels  256 us (97%)
  local copies, waits for them, and re-layouts  3.89 us (1%)
    pallas_call x1, Pallas kernels, body(): pl.pallas_call(block_kernel, out_shape=(jax.ShapeDtypeStruct((patches, ro...  256 us

profile of v8, /device:TPU:25, one launch (start us, length us, event | category | flops | bytes accessed | tf_op | source)
XLA Modules:
  0.0 262.3 jit_solution(10589807663451420772)
XLA Ops:
  0.6 1.1 slice.3
  1.7 0.1 reshape.20
  1.8 0.8 copy.19
  2.6 255.9 %shard_map.95 = (f32[2,24,3072]{2,1,0:T(8,128)}, bf16[2,16,2,24,128]{4,3,2,1,0:T(8,128)(2,1)}) custom-call(bf16[2,24,3072]{2,1,0:T(8,128)(2,1)} %hid.1, f32[4,1,768]{2,1,0:T(1,128)} %bitcast.20, f32[4,1,768]{2,1,0:T(1,128)} %bitcast.21, f32[4,1,768]{2,1,0:T(1,128)} %bitcast.22, f32[2,128]{1,0:T(2,128)} %bitcast.23, bf16[3,3072,128]{2,1,0:T(8,128)(2,1)} %bitcast.16, ...), custom_call_target="tpu_custom_call" | custom-call | tf_op jit(solution)/shard_map/pallas_call | solution.py:384
  258.5 1.8 convert_bitcast_fusion
  260.3 1.1 copy.16
  261.4 0.8 reshape.21
